TPU v7x, 256 devices: a whole 4x4x8 slice. The times are simulated.
256 devices in a mesh: row: 16 (over x, y_hi, core), col: 16 (over y_lo, z).
Axes of the slice: x: 4, y: 4 (y_hi: 2, y_lo: 2; y = y_hi * 2 + y_lo), z: 8, core: 2. Of those that a mesh axis runs over, the one named last changes fastest.
Arguments:
- query_in: bfloat16 [4096, 8192], P('row', 'col'), may hold values from -6 to 6
- key_in: bfloat16 [4096, 8192], P('row', 'col'), may hold values from -6 to 6
- value_in: bfloat16 [4096, 8192], P('row', 'col'), may hold values from -6 to 6
- filters: float32 [512, 128], P('col'), may hold values from -0.5 to 0.5
- out_weight: bfloat16 [8192, 8192], P('row', 'col'), may hold values from -0.0625 to 0.0625
- out_grad: bfloat16 [4096, 8192], P('row', 'col'), may hold values from -6 to 6
Outputs:
- mixed: bfloat16 [4096, 8192], P('row', 'col')
- query_grad: bfloat16 [4096, 8192], P('row', 'col')
- key_grad: bfloat16 [4096, 8192], P('row', 'col')
- value_grad: bfloat16 [4096, 8192], P('row', 'col')
- weight_grad: bfloat16 [8192, 8192], P('row', 'col')
- filter_grad: float32 [512, 128], P('col')
All inputs are finite; a program needn't handle non-finite values.
Results may differ from a plain program's by a relative error of at most 0.018.
Values may be sent and summed in bfloat16 or wider, within the bound.
A program may use at most 128 MiB of HBM per device.

v0:
```python
import math

import jax
import jax.numpy as jnp
from jax import lax
from jax.sharding import PartitionSpec as P


def from_behind(shard, axis, by):
    size = lax.axis_size(axis)
    pairs = [(i, i + by) for i in range(size) if 0 <= i + by < size]
    return lax.ppermute(shard, axis, pairs)


def toeplitz(taps, causal):
    groups, span = taps.shape
    if causal:
        template = jnp.concatenate(
            [
                jnp.zeros((groups, 1), jnp.float32),
                taps[:, ::-1],
                jnp.zeros((groups, span), jnp.float32),
            ],
            1,
        )
    else:
        template = jnp.concatenate([taps, jnp.zeros((groups, span + 1), jnp.float32)], 1)
    tiled = jnp.tile(template, (1, span))
    return tiled[:, : 2 * span * span].reshape(groups, span, 2 * span)


def windows(extended, span):
    count = (extended.shape[0] - span) // span
    first = extended[:-span].reshape(count, span, extended.shape[1])
    second = extended[span:].reshape(count, span, extended.shape[1])
    return jnp.concatenate([first, second], axis=1)


def convolve(matrix, extended, span, group):
    blocks = windows(extended, span)
    count, _, width = blocks.shape
    split = blocks.reshape(count, 2 * span, width // group, group)
    result = jnp.einsum("gts,bsgc->btgc", matrix, split, precision=lax.Precision.HIGHEST)
    return result.reshape(count * span, width)


def shards(query_in, key_in, value_in, filters, out_weight, out_grad):
    f32 = jnp.float32
    bf16 = jnp.bfloat16
    tokens, width = query_in.shape
    span = filters.shape[1]
    group = width // filters.shape[0]
    total_tokens = tokens * lax.axis_size("row")
    key32 = key_in.astype(f32)
    value32 = value_in.astype(f32)
    query32 = query_in.astype(f32)
    product = key32 * value32
    key_rim, value_rim = from_behind((key_in[-span:], value_in[-span:]), "row", 1)
    product_rim = key_rim.astype(f32) * value_rim.astype(f32)
    product_ext = jnp.concatenate([product_rim, product], 0)
    conv = convolve(toeplitz(filters, True), product_ext, span, group)
    gated = (query32 * conv).astype(bf16)
    panel = lax.all_gather(gated, "col", axis=1, tiled=True)
    weights = lax.all_gather(out_weight, "row", axis=0, tiled=True)
    mixed_sum = jnp.dot(panel, weights, preferred_element_type=f32)
    partial_value = lax.dot_general(
        out_grad, weights, (((1,), (1,)), ((), ())), preferred_element_type=f32
    )
    mixed = mixed_sum.astype(bf16)
    grad_gated = lax.psum_scatter(
        partial_value.astype(jnp.bfloat16), "col", scatter_dimension=1, tiled=True
    ).astype(jnp.float32)
    query_grad = (grad_gated * conv).astype(bf16)
    grad_conv = grad_gated * query32
    grad_rim = from_behind(grad_conv[:span].astype(jnp.bfloat16), "row", -1).astype(jnp.float32)
    grad_ext = jnp.concatenate([grad_conv, grad_rim], 0)
    grad_product = convolve(toeplitz(filters, False), grad_ext, span, group)
    key_grad = (grad_product * value32).astype(bf16)
    value_grad = (grad_product * key32).astype(bf16)
    count = tokens // span
    groups = width // group
    grad_blocks = grad_conv.reshape(count, span, groups, group)
    product_blocks = windows(product_ext, span).reshape(count, 2 * span, groups, group)
    corr = jnp.einsum(
        "btgc,bsgc->gts", grad_blocks, product_blocks, precision=lax.Precision.HIGHEST
    )
    flat = jnp.concatenate(
        [corr.reshape(groups, 2 * span * span), jnp.zeros((groups, span), f32)], 1
    )
    skewed = flat.reshape(groups, span, 2 * span + 1)[:, :, 1 : span + 1]
    local_taps = jnp.sum(skewed, axis=1)[:, ::-1]
    filter_grad = lax.psum(local_taps, "row") * (1.0 / math.sqrt(total_tokens * group))
    weight_sum = lax.psum_scatter(
        lax.dot_general(
            panel, out_grad, (((0,), (0,)), ((), ())), preferred_element_type=f32
        ).astype(jnp.bfloat16),
        "row",
        scatter_dimension=0,
        tiled=True,
    ).astype(jnp.float32)
    weight_grad = (weight_sum * (1.0 / math.sqrt(total_tokens))).astype(bf16)
    return (mixed, query_grad, key_grad, value_grad, weight_grad, filter_grad)


def solution(mesh):
    placed = (
        P("row", "col"),
        P("row", "col"),
        P("row", "col"),
        P("col", None),
        P("row", "col"),
        P("row", "col"),
    )
    return jax.shard_map(
        shards,
        mesh=mesh,
        in_specs=placed,
        out_specs=(
            P("row", "col"),
            P("row", "col"),
            P("row", "col"),
            P("row", "col"),
            P("row", "col"),
            P("col", None),
        ),
        check_vma=False,
    )
```

profile of v0, /device:TPU:1, one launch (start us, length us, event | category | flops | bytes accessed | tf_op | source)
XLA Modules:
  0.0 399.2 jit_solution(14120310710008545654)
XLA Ops:
  7.2 0.0 copy-start
  7.2 0.0 all-gather.5.cloned.1.call-start
  7.2 0.7 all-gather.5.cloned.1.call-update
  7.9 0.0 reduce-scatter.3.cloned.1.call-start
  8.0 84.8 %all-gather.5.cloned.1.call-done = bf16[8192,512]{1,0:T(8,128)(2,1)} async-done(((bf16[512,512]{1,0:T(8,128)(2,1)}), bf16[8192,512]{1,0:T(8,128)(2,1)}) %all-gather.5.cloned.1.call-update) | async-done | bytes 8388624 | tf_op jit(solution)/shard_map/all_gather | solution.py:64
  92.8 7.8 %convolution_convert_fusion.1 = bf16[256,8192]{1,0:T(8,128)(2,1)} fusion(bf16[256,512]{1,0:T(8,128)(2,1)S(1)} %copy-done, bf16[8192,512]{1,0:T(8,128)(2,1)} %all-gather.5.cloned.1.call-done), kind=kOutput, calls=%fused_computation.1 | convolution fusion | flops 2149580800 | bytes 12845056 | tf_op jit(solution)/shard_map/dot_general | solution.py:66
  100.6 0.0 reduce-scatter.3.cloned.1.call-update
  100.6 0.0 all-gather.3.cloned.1.call-start
  100.7 0.9 copy-done.6
  101.5 0.1 copy.15
  101.7 2.3 collective-permute-start
  104.0 0.1 copy.16
  104.2 2.1 collective-permute-start.1
  106.3 0.1 rev.6
  106.4 3.1 tile.20
  109.5 6.7 %tile.21 = f32[32,32896]{1,0:T(8,128)} reshape(f32[32,128,257]{2,1,0:T(8,128)} %tile.20) | data formatting | bytes 8421376 | tf_op jit(solution)/shard_map/tile | solution.py:28
  116.2 2.2 slice-done
  118.4 3.3 copy.37
  121.8 0.1 pad.8.clone
  121.9 0.1 maximum_maximum_fusion
  121.9 3.1 tile.8
  125.1 6.7 %tile.9 = f32[32,32896]{1,0:T(8,128)} reshape(f32[32,128,257]{2,1,0:T(8,128)} %tile.8) | data formatting | bytes 8421376 | tf_op jit(solution)/shard_map/tile | solution.py:28
  131.8 2.2 slice-done.1
  134.0 3.2 copy.35
  137.2 31.4 %reduce-scatter.3.cloned.1.call-done = bf16[256,512]{1,0:T(8,128)(2,1)} async-done(((bf16[256,8192]{1,0:T(8,128)(2,1)}), bf16[256,512]{1,0:T(8,128)(2,1)}) %reduce-scatter.3.cloned.1.call-update) | async-done | bytes 262160 | tf_op jit(solution)/shard_map/reduce_scatter | solution.py:70
  168.6 1.0 convert_multiply_fusion
  169.6 0.7 slice.42
  170.3 13.6 %collective-permute-start.2 = (bf16[128,512]{1,0:T(8,128)(2,1)}, bf16[128,512]{1,0:T(8,128)(2,1)S(1)}, u32[]{:S(2)}, u32[]{:S(2)}) collective-permute-start(bf16[128,512]{1,0:T(8,128)(2,1)} %slice.42), channel_id=1, source_target_pairs={{16,0},{32,16},{48,32},{64,48},{80,64},{96,80},{112,96},{128,112},... | collective-permute-start | bytes 393224 | tf_op jit(solution)/shard_map/ppermute | solution.py:12
  183.9 0.0 collective-permute-done
  183.9 0.0 collective-permute-done.1
  184.0 0.2 copy.24
  184.2 0.3 concatenate.37
  184.5 4.9 %collective-permute-done.2 = bf16[128,512]{1,0:T(8,128)(2,1)S(1)} collective-permute-done((bf16[128,512]{1,0:T(8,128)(2,1)}, bf16[128,512]{1,0:T(8,128)(2,1)S(1)}, u32[]{:S(2)}, u32[]{:S(2)}) %collective-permute-start.2) | collective-permute-done | bytes 131104 | tf_op jit(solution)/shard_map/ppermute | solution.py:12
  189.4 0.2 copy.25
  189.6 0.3 concatenate.39
  190.0 5.9 %fusion.7 = f32[2,128,32,16]{1,3,0,2:T(8,128)S(1)} fusion(f32[32,128,256,1]{2,1,0,3:T(8,128)} %bitcast.60, f32[2,128,32,16]{1,3,0,2:T(8,128)S(1)} %copy.27, f32[2,128,32,16]{1,3,0,2:T(8,128)S(1)} %copy.26), kind=kOutput, calls=%fused_computation.8 | convolution fusion | flops 402915328 | bytes 5767168 | tf_op jit(solution)/shard_map/gts,bsgc->btgc/dot_general | solution.py:43
  195.9 0.3 copy.28
  196.2 0.9 fusion.14
  197.1 0.3 concatenate.34
  197.4 0.3 concatenate.33
  197.7 0.1 copy_dynamic-update-slice_fusion.1
  197.7 0.1 copy_dynamic-update-slice_fusion
  197.8 5.9 %fusion.4 = f32[2,128,32,16]{1,3,0,2:T(8,128)S(1)} fusion(f32[2,256,32,16]{1,3,0,2:T(8,128)S(1)} %copy_dynamic-update-slice_fusion, f32[32,128,256,1]{2,1,0,3:T(8,128)} %bitcast.59), kind=kOutput, calls=%fused_computation.7 | convolution fusion | flops 402653184 | bytes 5767168 | tf_op jit(solution)/shard_map/gts,bsgc->btgc/dot_general | solution.py:43
  203.8 0.3 copy.21
  204.1 0.2 copy.22
  204.3 0.9 fusion.16
  205.2 0.0 all-gather.3.cloned.1.call-update
  205.2 0.3 reduce-scatter.5.cloned.1.call-start
  205.5 60.9 %all-gather.3.cloned.1.call-done = bf16[256,8192]{1,0:T(8,128)(2,1)} async-done(((bf16[256,512]{1,0:T(8,128)(2,1)}), bf16[256,8192]{1,0:T(8,128)(2,1)}) %all-gather.3.cloned.1.call-update) | async-done | bytes 4194320 | tf_op jit(solution)/shard_map/all_gather | solution.py:63
  266.4 7.8 %convolution_convert_fusion = bf16[8192,512]{1,0:T(8,128)(2,1)} fusion(bf16[256,8192]{1,0:T(8,128)(2,1)} %all-gather.3.cloned.1.call-done, bf16[256,512]{1,0:T(8,128)(2,1)S(1)} %copy-done), kind=kOutput, calls=%fused_computation | convolution fusion | flops 2151677952 | bytes 12845056 | tf_op jit(solution)/shard_map/dot_general | solution.py:94
  274.2 0.0 reduce-scatter.5.cloned.1.call-update
  274.3 3.5 fusion.18
  277.8 2.4 copy.39
  280.2 2.3 concatenate.42
  282.5 8.1 %reshape.61 = f32[32,128,257]{2,1,0:T(8,128)} reshape(f32[32,32896]{1,0:T(8,128)} %concatenate.42) | data formatting | bytes 8421376 | tf_op jit(solution)/shard_map/reshape | solution.py:90
  290.6 2.9 slice_reduce_fusion
  293.5 0.1 rev.7
  293.6 0.8 copy.30
  294.4 0.8 copy.31
  295.3 70.9 %psum.7 = f32[32,128]{1,0:T(8,128)S(1)} all-reduce(f32[32,128]{1,0:T(8,128)S(1)} %rev.7), channel_id=1, replica_groups=mesh['row'=16,'col'=16] {'row'}, use_global_device_ids=true, to_apply=%region_3.0 | all-reduce | flops 4096 | bytes 32768 | tf_op jit(solution)/shard_map/psum | solution.py:92
  366.2 0.6 broadcast_multiply_fusion
  366.8 7.7 %convolution_convert_fusion.2 = bf16[256,512]{1,0:T(8,128)(2,1)} fusion(bf16[256,8192]{1,0:T(8,128)(2,1)} %all-gather.3.cloned.1.call-done, bf16[8192,512]{1,0:T(8,128)(2,1)} %all-gather.5.cloned.1.call-done), kind=kOutput, calls=%fused_computation.9 | convolution fusion | flops 2147614720 | bytes 12845056 | tf_op jit(solution)/shard_map/dot_general | solution.py:65
  374.5 16.3 %reduce-scatter.5.cloned.1.call-done = bf16[512,512]{1,0:T(8,128)(2,1)} async-done(((bf16[8192,512]{1,0:T(8,128)(2,1)}), bf16[512,512]{1,0:T(8,128)(2,1)}) %reduce-scatter.5.cloned.1.call-update) | async-done | bytes 524304 | tf_op jit(solution)/shard_map/reduce_scatter | solution.py:93
  390.8 1.9 multiply_convert_fusion
  (30 shorter events, 0.3 us)
Async XLA Ops:
  7.2 85.6 %copy-start = (bf16[256,512]{1,0:T(8,128)(2,1)S(1)}, bf16[256,512]{1,0:T(8,128)(2,1)}, u32[]{:S(2)}) copy-start(bf16[256,512]{1,0:T(8,128)(2,1)} %param.11) | copy-start | bytes 786436
  7.2 85.6 %all-gather.5.cloned.1.call-start = ((), (), s32[]{:S(2)}) async-start(), calls=%async_computation.3 | async-start | bytes 8912896 | tf_op jit(solution)/shard_map/all_gather | solution.py:64
  7.9 160.7 %reduce-scatter.3.cloned.1.call-start = ((), (), s32[]{:S(2)}) async-start(), calls=%async_computation.4 | async-start | bytes 4456448 | tf_op jit(solution)/shard_map/reduce_scatter | solution.py:70
  100.6 0.9 copy-start.6
  100.6 3.4 copy-start.7
  100.6 5.7 %copy-start.8 = (f32[32,128]{1,0:T(8,128)S(1)}, f32[32,128]{1,0:T(8,128)}, u32[]{:S(2)}) copy-start(f32[32,128]{1,0:T(8,128)} %param.9) | copy-start | bytes 49156
  100.6 165.8 %all-gather.3.cloned.1.call-start = ((), (), s32[]{:S(2)}) async-start(), calls=%async_computation.2 | async-start | bytes 4456448 | tf_op jit(solution)/shard_map/all_gather | solution.py:63
  101.7 82.2 %collective-permute-start = (bf16[128,512]{0,1:T(8,128)(2,1)S(1)}, bf16[128,512]{0,1:T(8,128)(2,1)S(1)}, u32[]{:S(2)}, u32[]{:S(2)}) collective-permute-start(bf16[128,512]{0,1:T(8,128)(2,1)S(1)} %slice.34), channel_id=1, source_target_pairs={{0,16},{16,32},{32,48},{48,64},{64,80},{80,96},{96,112},{112,128},... | collective-permute-start | bytes 393224 | tf_op jit(solution)/shard_map/ppermute | solution.py:12
  104.2 79.8 %collective-permute-start.1 = (bf16[128,512]{0,1:T(8,128)(2,1)S(1)}, bf16[128,512]{0,1:T(8,128)(2,1)S(1)}, u32[]{:S(2)}, u32[]{:S(2)}) collective-permute-start(bf16[128,512]{0,1:T(8,128)(2,1)S(1)} %slice.35), channel_id=1, source_target_pairs={{0,16},{16,32},{32,48},{48,64},{64,80},{80,96},{96,112},{112,128},... | collective-permute-start | bytes 393224 | tf_op jit(solution)/shard_map/ppermute | solution.py:12
  116.2 2.2 slice-start
  131.8 2.2 slice-start.1
  134.0 34.6 %copy-start.2 = (bf16[256,512]{1,0:T(8,128)(2,1)S(1)}, bf16[256,512]{1,0:T(8,128)(2,1)}, u32[]{:S(2)}) copy-start(bf16[256,512]{1,0:T(8,128)(2,1)} %param.6) | copy-start | bytes 786436
  170.3 19.1 %collective-permute-start.2 = (bf16[128,512]{1,0:T(8,128)(2,1)}, bf16[128,512]{1,0:T(8,128)(2,1)S(1)}, u32[]{:S(2)}, u32[]{:S(2)}) collective-permute-start(bf16[128,512]{1,0:T(8,128)(2,1)} %slice.42), channel_id=1, source_target_pairs={{16,0},{32,16},{48,32},{64,48},{80,64},{96,80},{112,96},{128,112},... | collective-permute-start | bytes 393224 | tf_op jit(solution)/shard_map/ppermute | solution.py:12
  197.8 6.5 %copy-start.3 = (bf16[256,512]{1,0:T(8,128)(2,1)S(1)}, bf16[256,512]{1,0:T(8,128)(2,1)}, u32[]{:S(2)}) copy-start(bf16[256,512]{1,0:T(8,128)(2,1)} %reduce-scatter.3.cloned.1.call-done) | copy-start | bytes 786436
  205.2 185.5 %reduce-scatter.5.cloned.1.call-start = ((), (), s32[]{:S(2)}) async-start(), calls=%async_computation.5 | async-start | bytes 8912896 | tf_op jit(solution)/shard_map/reduce_scatter | solution.py:93
  282.5 11.1 %copy-start.5 = (bf16[256,512]{0,1:T(8,128)(2,1)S(1)}, bf16[256,512]{0,1:T(8,128)(2,1)}, u32[]{:S(2)}) copy-start(bf16[256,512]{0,1:T(8,128)(2,1)} %get-tuple-element.13) | copy-start | bytes 786436
  282.5 11.9 %copy-start.4 = (bf16[256,512]{0,1:T(8,128)(2,1)S(1)}, bf16[256,512]{0,1:T(8,128)(2,1)}, u32[]{:S(2)}) copy-start(bf16[256,512]{0,1:T(8,128)(2,1)} %get-tuple-element.12) | copy-start | bytes 786436
  366.8 25.9 %copy-start.1 = (bf16[256,512]{1,0:T(8,128)(2,1)S(1)}, bf16[256,512]{1,0:T(8,128)(2,1)}, u32[]{:S(2)}) copy-start(bf16[256,512]{1,0:T(8,128)(2,1)} %param.11) | copy-start | bytes 786436
Sparse Core Ops, SparseCore 0:
  10.7 82.0 all-gather.4
  100.7 67.8 reduce-scatter.2
  205.4 61.0 all-gather.2
  274.4 116.3 reduce-scatter.4
where the time goes:
time: 400 us; the launch traced here: 399 us
  waiting for transfers between devices  199 us (50%)
  blocking collectives  70.9 us (18%)
  local copies, waits for them, and re-layouts  49.7 us (12%)
  matrix products  38.7 us (10%)
  starting transfers between devices  18.4 us (5%)
  between operations  14.1 us (4%)
  other arithmetic  8.46 us (2%)
    all_gather x1, waiting for transfers between devices, shards(): weights = lax.all_gather(out_weight, 'row', axis=0, tiled=True)  84.8 us
    psum x1, blocking collectives, shards(): lax.psum(local_taps, 'row') * (1.0 / math.sqrt(total_tokens * group))  70.9 us
    all_gather x1, waiting for transfers between devices, shards(): panel = lax.all_gather(gated, 'col', axis=1, tiled=True)  60.9 us
    reduce_scatter x1, waiting for transfers between devices, shards(): lax.psum_scatter(partial_value.astype(jnp.bfloat16), 'col', scatter_dimen...  31.4 us
    another operation x4, local copies, waits for them, and re-layouts, toeplitz(): tiled = jnp.tile(template, (1, span))  19.6 us
    ppermute x3, starting transfers between devices, from_behind(): return lax.ppermute(shard, axis, pairs)  18.1 us
    reduce_scatter x1, waiting for transfers between devices, shards(): lax.psum_scatter(lax.dot_general(panel, out_grad, (((0,), (0,)), ((), ())...  16.3 us
    unnamed x27, local copies, waits for them, and re-layouts  12 us
  transfers between devices with their start and end apart: 7, of which 5 were waited for; matrix products, arithmetic and copies ran while one was open for 15% of the time, Pallas kernels for 0%

commit v1 on v0

v1 whole, which is shorter than its diff:
```python
import math

import jax
import jax.numpy as jnp
from jax import lax
from jax.experimental import pallas as pl
from jax.experimental.pallas import tpu as pltpu
from jax.sharding import PartitionSpec as P

F32 = jnp.float32
BF16 = jnp.bfloat16
MESH = pl.DeviceIdType.MESH
NT = (((1,), (1,)), ((), ()))
TN = (((0,), (0,)), ((), ()))
NN = (((1,), (0,)), ((), ()))


def dot(a, b, dims=NN):
    return lax.dot_general(a, b, dims, preferred_element_type=F32)


def split(x):
    high = x.astype(BF16)
    return high, (x - high.astype(F32)).astype(BF16)


def kernel(
    q_ref, k_ref, v_ref, f_ref, fr_ref, w_ref, og_ref,
    mixed_ref, qg_ref, kg_ref, vg_ref, wg_ref, fg_ref,
    k_rim, v_rim, g_send, g_rim,
    t_hi, t_lo, a_hi, a_lo, x_hi, x_lo, conv, gc,
    wp, gp, pb, rp, pair, wb, sb, xfar, xnear, yb,
    taps, taps_in, acc, ss, rs, ls,
):
    tok, wid = q_ref.shape
    span = f_ref.shape[1]
    groups = f_ref.shape[0]
    group = wid // groups
    lanes = 128
    tiles = wid // lanes
    per = lanes // group
    half = tok // 2
    whalf = wid // 2

    r = lax.axis_index("row")
    c = lax.axis_index("col")
    x, yh, core = r // 4, lax.rem(r // 2, 2), lax.rem(r, 2)
    yl, z = c // 8, lax.rem(c, 8)

    def rowid(dx, flip_y, flip_core):
        yy = 1 - yh if flip_y else yh
        cc = 1 - core if flip_core else core
        return lax.rem(x + dx + 4, 4) * 4 + yy * 2 + cc

    def colid(dz, flip_y):
        yy = 1 - yl if flip_y else yl
        return yy * 8 + lax.rem(z + dz + 8, 8)

    sib = (rowid(0, 0, 1), c)
    ytwo = (rowid(0, 1, 0), c)
    xdev = {1: (rowid(1, 0, 0), c), -1: (rowid(-1, 0, 0), c)}
    zdev = {1: (r, colid(1, 0)), -1: (r, colid(-1, 0))}
    ypair = (r, colid(0, 1))
    after = (lax.rem(r + 1, 16), c)
    before = (lax.rem(r + 15, 16), c)

    barrier = pltpu.get_barrier_semaphore()
    peers = [sib, ytwo, xdev[1], xdev[-1], zdev[1], zdev[-1], ypair, after, before]
    for peer in peers:
        pl.semaphore_signal(barrier, inc=1, device_id=peer, device_id_type=MESH)
    pl.semaphore_wait(barrier, len(peers))

    names = {}
    started = []

    def slot(name):
        return names.setdefault(name, len(names))

    def desc(src, dst, name, dev):
        n = name if not isinstance(name, str) else slot(name)
        return pltpu.make_async_remote_copy(
            src_ref=src, dst_ref=dst, send_sem=ss.at[n], recv_sem=rs.at[n],
            device_id=dev, device_id_type=MESH,
        )

    def send(src, dst, name, dev):
        copy = desc(src, dst, name, dev)
        copy.start()
        started.append(copy)

    def recv(dst, name, dev):
        desc(dst, dst, name, dev).wait_recv()

    def add_into(dst, src):
        step = 64

        def body(i, carry):
            rows = pl.ds(pl.multiple_of(i * step, step), step)
            dst[rows, :] = (dst[rows, :].astype(F32) + src[rows, :].astype(F32)).astype(BF16)
            return carry

        lax.fori_loop(0, dst.shape[0] // step, body, 0)

    send(k_ref.at[pl.ds(tok - span, span)], k_rim, "hk", after)
    send(v_ref.at[pl.ds(tok - span, span)], v_rim, "hv", after)
    send(w_ref, wp.at[r], "w_y", ytwo)
    for s in (1, -1):
        send(w_ref, wp.at[r], f"w_x{s}", xdev[s])
    send(w_ref, wp.at[r], "w_s00", sib)
    own = pltpu.make_async_copy(w_ref, wp.at[r], ls.at[0])
    own.start()

    def shear(row, shift):
        wide = jnp.concatenate([row, jnp.zeros((1, span), F32)], axis=1)
        wide = jnp.broadcast_to(wide, (span, 2 * span))
        return pltpu.roll(wide, shift, 1, stride=1, stride_axis=0)

    def build(source, high_ref, low_ref, shift):
        def body(g, carry):
            rows = pl.ds(pl.multiple_of(g * span, span), span)
            high, low = split(shear(source[pl.ds(g, 1), :], shift))
            high_ref[rows, :] = high
            low_ref[rows, :] = low
            return carry

        lax.fori_loop(0, groups, body, 0)

    lane_group = lax.broadcasted_iota(jnp.int32, (span, 2 * lanes), 1)
    lane_group = lax.rem(lane_group, lanes) // group

    def pick(full):
        out = full[0:span]
        for g in range(1, per):
            out = jnp.where(lane_group == g, full[g * span:(g + 1) * span], out)
        return out

    def two(ref, cols):
        return jnp.concatenate(
            [ref[pl.ds(0, 2 * span), cols], ref[pl.ds(span, 2 * span), cols]], axis=1
        )

    def filtered(high_ref, low_ref, j, xh, xl):
        rows = pl.ds(pl.multiple_of(j * per * span, per * span), per * span)
        mh = high_ref[rows, :]
        full = dot(mh, xh) + dot(mh, xl) + dot(low_ref[rows, :], xh)
        return pick(full)

    build(fr_ref, t_hi, t_lo, 1)
    high, low = split(k_ref[...].astype(F32) * v_ref[...].astype(F32))
    x_hi[pl.ds(span, tok), :] = high
    x_lo[pl.ds(span, tok), :] = low
    recv(k_rim, "hk", before)
    recv(v_rim, "hv", before)
    rim = k_rim[...].astype(F32) * v_rim[...].astype(F32)
    high, low = split(jnp.where(r > 0, rim, 0.0))
    x_hi[pl.ds(0, span), :] = high
    x_lo[pl.ds(0, span), :] = low

    def forward(j, carry):
        cols = pl.ds(pl.multiple_of(j * lanes, lanes), lanes)
        out = filtered(t_hi, t_lo, j, two(x_hi, cols), two(x_lo, cols))
        for b in range(2):
            rows = pl.ds(b * span, span)
            part = out[:, b * lanes:(b + 1) * lanes]
            conv[rows, cols] = part
            gp[c, rows, cols] = (q_ref[rows, cols].astype(F32) * part).astype(BF16)
        return carry

    lax.fori_loop(0, tiles, forward, 0)

    send(gp.at[c], gp.at[c], "g_y", ypair)
    for s in (1, -1):
        send(gp.at[c], gp.at[c], f"g_{s}_0_1", zdev[s])

    def w_half(s):
        return pl.ds(0 if s == 1 else whalf, whalf)

    def g_half(s):
        return pl.ds(0 if s == 1 else half, half)

    def w_near(flip):
        for s in (1, -1):
            blk = rowid(-s, flip, 0)
            name = f"w_x{s}" if not flip else f"w_yx{s}"
            recv(wp.at[blk], name, xdev[-s])
            rows = w_half(s)
            send(wp.at[blk, rows], wp.at[blk, rows], f"w_far{s}_{flip}", xdev[s])
            send(wp.at[blk], wp.at[blk], f"w_s{s}{flip}", sib)

    def g_step(flip, dist):
        for s in (1, -1):
            blk = colid(-s * dist, flip)
            recv(gp.at[blk], f"g_{s}_{flip}_{dist}", zdev[-s])
            if dist < 3:
                send(gp.at[blk], gp.at[blk], f"g_{s}_{flip}_{dist + 1}", zdev[s])
            else:
                rows = g_half(s)
                send(gp.at[blk, rows], gp.at[blk, rows], f"g_{s}_{flip}_4", zdev[s])

    w_near(0)
    blk = colid(0, 1)
    recv(gp.at[blk], "g_y", ypair)
    for s in (1, -1):
        send(gp.at[blk], gp.at[blk], f"g_{s}_1_1", zdev[s])
    g_step(0, 1)
    build(f_ref, a_hi, a_lo, 0)
    blk = rowid(0, 1, 0)
    recv(wp.at[blk], "w_y", ytwo)
    for s in (1, -1):
        send(wp.at[blk], wp.at[blk], f"w_yx{s}", xdev[s])
    send(wp.at[blk], wp.at[blk], "w_s01", sib)
    g_step(1, 1)
    g_step(0, 2)
    w_near(1)
    g_step(1, 2)
    g_step(0, 3)
    for flip in (0, 1):
        blk = rowid(2, flip, 0)
        for s in (1, -1):
            rows = w_half(s)
            recv(wp.at[blk, rows], f"w_far{s}_{flip}", xdev[-s])
        send(wp.at[blk], wp.at[blk], f"w_s2{flip}", sib)
    g_step(1, 3)
    own.wait()
    for flip in (0, 1):
        recv(wp.at[rowid(0, flip, 1)], f"w_s0{flip}", sib)
        for s in (1, -1):
            recv(wp.at[rowid(-s, flip, 1)], f"w_s{s}{flip}", sib)
        recv(wp.at[rowid(2, flip, 1)], f"w_s2{flip}", sib)

    def partial(i, carry):
        pb[i] = dot(og_ref[...], wp[i], NT).astype(BF16)
        return carry

    lax.fori_loop(0, 16, partial, 0)

    def p_send(flip, dist):
        for n, s in enumerate((1, -1)):
            dest = colid(s * dist, flip)
            if dist == 4:
                rows = g_half(s)
                send(pb.at[dest, rows], rp.at[n, flip, 3, rows], f"p_{s}_{flip}_4", zdev[s])
                continue
            if dist == 3:
                rows = g_half(s)
                recv(rp.at[n, flip, 3, rows], f"p_{s}_{flip}_4", zdev[-s])
                add_into(pb.at[dest, rows], rp.at[n, flip, 3, rows])
            else:
                recv(rp.at[n, flip, dist], f"p_{s}_{flip}_{dist + 1}", zdev[-s])
                add_into(pb.at[dest], rp.at[n, flip, dist])
            send(pb.at[dest], rp.at[n, flip, dist - 1], f"p_{s}_{flip}_{dist}", zdev[s])

    p_send(1, 4)
    p_send(0, 4)
    for flip in (0, 1):
        blk = colid(4, flip)
        for s in (1, -1):
            rows = g_half(s)
            recv(gp.at[blk, rows], f"g_{s}_{flip}_4", zdev[-s])

    order = [(2, 1), (2, 0), (1, 1), (-1, 1), (1, 0), (-1, 0), (0, 1), (0, 0)]
    sib_base = slot("s_0")
    for i in range(1, 8):
        slot(f"s_{i}")

    def order_row(i, cc):
        dx = jnp.where(i < 2, 2, jnp.where(i >= 6, 0, jnp.where(lax.rem(i, 2) == 0, 1, 3)))
        flip = jnp.where(i < 2, 1 - i, jnp.where(i >= 6, 7 - i, jnp.where(i < 4, 1, 0)))
        yy = lax.rem(yh + flip, 2)
        return lax.rem(x + dx, 4) * 4 + yy * 2 + cc

    def for_sib(i, carry):
        dest = order_row(i, 1 - core)
        wb[dest] = dot(gp[dest], og_ref[...], TN).astype(BF16)
        desc(wb.at[dest], sb.at[i], sib_base + i, sib).start()
        return carry

    def for_own(i, carry):
        dest = order_row(i, core)
        part = dot(gp[dest], og_ref[...], TN)
        desc(sb.at[i], sb.at[i], sib_base + i, sib).wait_recv()
        wb[dest] = (part + sb[i].astype(F32)).astype(BF16)
        return carry

    def wx_far(flip):
        for n, s in enumerate((1, -1)):
            dest = rowid(2, flip, 0)
            rows = w_half(s)
            send(wb.at[dest, rows], xfar.at[n, flip], f"x_far{s}_{flip}", xdev[s])

    def wx_near(flip):
        for n, s in enumerate((1, -1)):
            dest = rowid(s, flip, 0)
            rows = w_half(s)
            recv(xfar.at[n, flip], f"x_far{s}_{flip}", xdev[-s])
            add_into(wb.at[dest, rows], xfar.at[n, flip])
            send(wb.at[dest], xnear.at[n, flip], f"x_near{s}_{flip}", xdev[s])

    lax.fori_loop(0, 8, for_sib, 0)
    p_send(1, 3)
    p_send(0, 3)
    lax.fori_loop(0, 2, for_own, 0)
    wx_far(1)
    wx_far(0)
    lax.fori_loop(2, 8, for_own, 0)
    p_send(1, 2)
    p_send(0, 2)
    wx_near(1)
    wx_near(0)

    acc[...] = jnp.zeros_like(acc)

    def mix(i, carry):
        acc[...] += dot(gp[i], wp[i])
        return carry

    lax.fori_loop(0, 8, mix, 0)
    p_send(1, 1)
    p_send(0, 1)
    lax.fori_loop(8, 16, mix, 0)
    mixed_ref[...] = acc[...].astype(BF16)

    def w_total(flip):
        dest = rowid(0, flip, 0)
        for n, s in enumerate((1, -1)):
            recv(xnear.at[n, flip], f"x_near{s}_{flip}", xdev[-s])
            add_into(wb.at[dest], xnear.at[n, flip])

    w_total(1)
    send(wb.at[rowid(0, 1, 0)], yb, "x_y", ytwo)

    blk = colid(0, 1)
    for n, s in enumerate((1, -1)):
        recv(rp.at[n, 1, 0], f"p_{s}_1_1", zdev[-s])
        add_into(pb.at[blk], rp.at[n, 1, 0])
    send(pb.at[blk], pair, "p_y", ypair)
    for n, s in enumerate((1, -1)):
        recv(rp.at[n, 0, 0], f"p_{s}_0_1", zdev[-s])
    recv(pair, "p_y", ypair)
    step = 64

    def gradients(i, carry):
        rows = pl.ds(pl.multiple_of(i * step, step), step)
        total = pb[c, rows, :].astype(F32) + rp[0, 0, 0, rows, :].astype(F32)
        total += rp[1, 0, 0, rows, :].astype(F32) + pair[rows, :].astype(F32)
        qg_ref[rows, :] = (total * conv[rows, :]).astype(BF16)
        grad = total * q_ref[rows, :].astype(F32)
        gc[rows, :] = grad
        return carry

    lax.fori_loop(0, tok // step, gradients, 0)
    g_send[...] = gc[pl.ds(0, span), :].astype(BF16)
    send(g_send, g_rim, "g_rim", before)

    def corr(j, carry):
        cols = pl.ds(pl.multiple_of(j * lanes, lanes), lanes)
        grad = jnp.concatenate([gc[pl.ds(0, span), cols], gc[pl.ds(span, span), cols]], axis=1)
        masked = jnp.concatenate(
            [jnp.where(lane_group == g, grad, 0.0) for g in range(per)], axis=0
        )
        gh, gl = split(masked)
        xh = two(x_hi, cols)
        xl = two(x_lo, cols)
        full = dot(gh, xh, NT) + dot(gh, xl, NT) + dot(gl, xh, NT)
        for g in range(per):
            block = full[g * span:(g + 1) * span]
            size = span
            while size > 8:
                size //= 2
                block = block[0:size] + pltpu.roll(block[size:2 * size], 2 * span - size, 1)
            sub = lax.broadcasted_iota(jnp.int32, (8, 2 * span), 0)
            for bit in (4, 2, 1):
                moved = pltpu.roll(block, 2 * span - bit, 1)
                block = jnp.where((sub // bit) % 2 == 1, moved, block)
            line = jnp.sum(block, axis=0, keepdims=True)
            taps[pl.ds(j * per + g, 1), :] = line
        return carry

    lax.fori_loop(0, tiles, corr, 0)

    recv(g_rim, "g_rim", after)
    own_taps = taps_in.at[0]
    own_taps[...] = taps[:, pl.ds(0, 2 * span)][:, 1:span + 1]
    odd = lax.rem(x, 2)
    hop_a = (lax.rem(x + 1 - 2 * odd + 4, 4) * 4 + yh * 2 + core, c)
    hop_b = (lax.rem(x - 1 + 2 * odd + 4, 4) * 4 + yh * 2 + core, c)
    hops = [sib, hop_a, hop_b, ytwo]

    def backward(j, carry):
        cols = pl.ds(pl.multiple_of(j * lanes, lanes), lanes)
        rimv = jnp.where(r < 15, g_rim[:, cols].astype(F32), 0.0)
        lower = gc[pl.ds(0, span), cols]
        upper = gc[pl.ds(span, span), cols]
        ext = jnp.concatenate(
            [jnp.concatenate([lower, upper], axis=0), jnp.concatenate([upper, rimv], axis=0)],
            axis=1,
        )
        xh, xl = split(ext)
        out = filtered(a_hi, a_lo, j, xh, xl)
        for b in range(2):
            rows = pl.ds(b * span, span)
            part = out[:, b * lanes:(b + 1) * lanes]
            kg_ref[rows, cols] = (part * v_ref[rows, cols].astype(F32)).astype(BF16)
            vg_ref[rows, cols] = (part * k_ref[rows, cols].astype(F32)).astype(BF16)
        return carry

    for n, hop in enumerate(hops):
        send(taps_in.at[2 * n], taps_in.at[2 * n + 1], f"t_{n}", hop)
        lax.fori_loop(n, n + 1, backward, 0)
        recv(taps_in.at[2 * n + 1], f"t_{n}", hop)
        taps_in[2 * n + 2] = taps_in[2 * n] + taps_in[2 * n + 1]
    fg_ref[...] = taps_in[8] * (1.0 / math.sqrt(tok * 16 * group))

    w_total(0)
    recv(yb, "x_y", ytwo)
    final = wb.at[r]
    scale = 1.0 / math.sqrt(tok * 16)

    def finish(i, carry):
        rows = pl.ds(pl.multiple_of(i * step, step), step)
        wg_ref[rows, :] = (
            (final[rows, :].astype(F32) + yb[rows, :].astype(F32)) * scale
        ).astype(BF16)
        return carry

    lax.fori_loop(0, wid // step, finish, 0)

    for copy in started:
        copy.wait_send()

    def drain(i, carry):
        desc(wb.at[0], sb.at[i], sib_base + i, sib).wait_send()
        return carry

    lax.fori_loop(0, 8, drain, 0)
    assert len(names) <= ss.shape[0], len(names)


def shards(query_in, key_in, value_in, filters, out_weight, out_grad):
    tok, wid = query_in.shape
    groups, span = filters.shape
    act = jax.ShapeDtypeStruct((tok, wid), BF16)
    vmem = pl.BlockSpec(memory_space=pltpu.VMEM)
    sems = 96
    mixed, qg, kg, vg, wg, fg = pl.pallas_call(
        kernel,
        out_shape=(
            act, act, act, act,
            jax.ShapeDtypeStruct((wid, wid), BF16),
            jax.ShapeDtypeStruct((groups, span), F32),
        ),
        in_specs=[vmem] * 7,
        out_specs=[vmem] * 6,
        scratch_shapes=[
            pltpu.VMEM((span, wid), BF16),
            pltpu.VMEM((span, wid), BF16),
            pltpu.VMEM((span, wid), BF16),
            pltpu.VMEM((span, wid), BF16),
            pltpu.VMEM((groups * span, 2 * span), BF16),
            pltpu.VMEM((groups * span, 2 * span), BF16),
            pltpu.VMEM((groups * span, 2 * span), BF16),
            pltpu.VMEM((groups * span, 2 * span), BF16),
            pltpu.VMEM((span + tok, wid), BF16),
            pltpu.VMEM((span + tok, wid), BF16),
            pltpu.VMEM((tok, wid), F32),
            pltpu.VMEM((tok, wid), F32),
            pltpu.VMEM((16, wid, wid), BF16),
            pltpu.VMEM((16, tok, wid), BF16),
            pltpu.VMEM((16, tok, wid), BF16),
            pltpu.VMEM((2, 2, 4, tok, wid), BF16),
            pltpu.VMEM((tok, wid), BF16),
            pltpu.VMEM((16, wid, wid), BF16),
            pltpu.VMEM((8, wid, wid), BF16),
            pltpu.VMEM((2, 2, wid // 2, wid), BF16),
            pltpu.VMEM((2, 2, wid, wid), BF16),
            pltpu.VMEM((wid, wid), BF16),
            pltpu.VMEM((groups, 2 * span), F32),
            pltpu.VMEM((9, groups, span), F32),
            pltpu.VMEM((tok, wid), F32),
            pltpu.SemaphoreType.DMA((sems,)),
            pltpu.SemaphoreType.DMA((sems,)),
            pltpu.SemaphoreType.DMA((1,)),
        ],
        compiler_params=pltpu.CompilerParams(
            collective_id=0, has_side_effects=True, vmem_limit_bytes=67_000_000
        ),
    )(query_in, key_in, value_in, filters, filters[:, ::-1], out_weight, out_grad)
    return mixed, qg, kg, vg, wg, fg[:, ::-1]


def solution(mesh):
    placed = (
        P("row", "col"),
        P("row", "col"),
        P("row", "col"),
        P("col", None),
        P("row", "col"),
        P("row", "col"),
    )
    return jax.shard_map(
        shards,
        mesh=mesh,
        in_specs=placed,
        out_specs=(
            P("row", "col"),
            P("row", "col"),
            P("row", "col"),
            P("row", "col"),
            P("row", "col"),
            P("col", None),
        ),
        check_vma=False,
    )
```

time: 400 us -> 146 us (0.36)
  waiting for transfers between devices: 199 us -> 0 us
  Pallas kernels: 0 us -> 136 us
  blocking collectives: 70.9 us -> 0 us
  local copies, waits for them, and re-layouts: 49.7 us -> 7.75 us
  matrix products: 38.7 us -> 0 us
  starting transfers between devices: 18.4 us -> 0 us
  between operations: 14.1 us -> 0.65 us
  other arithmetic: 8.46 us -> 0 us
    all_gather x2 -> x0, waiting for transfers between devices: 146 us -> none  [the longest x1 84.8 us: shards(): weights = lax.all_gather(out_weight, 'row', axis=0, tiled=True)]
    pallas_call x0 -> x1, Pallas kernels: none -> 136 us  [shards(): pl.pallas_call(kernel, out_shape=(act, act, act, act, jax.ShapeDtypeStruc...]
    psum x1 -> x0, blocking collectives: 70.9 us -> none  [shards(): lax.psum(local_taps, 'row') * (1.0 / math.sqrt(total_tokens * group))]
    reduce_scatter x2 -> x0, waiting for transfers between devices: 47.6 us -> none  [the longest x1 31.4 us: shards(): lax.psum_scatter(partial_value.astype(jnp.bfloat16), 'col', scatter_dimen...]
    dot_general x6 -> x0, matrix products: 38.7 us -> none  [the longest x2 11.9 us: convolve(): jnp.einsum('gts,bsgc->btgc', matrix, split, precision=lax.Precision.HIGHEST)]
    another operation x5 -> x0, local copies, waits for them, and re-layouts: 19.6 us -> none  [the longest x4 19.6 us: toeplitz(): tiled = jnp.tile(template, (1, span))]
    ppermute x3 -> x0, starting transfers between devices: 18.1 us -> none  [from_behind(): return lax.ppermute(shard, axis, pairs)]
    reshape x2 -> x0, local copies, waits for them, and re-layouts: 8.26 us -> none  [the longest x1 8.07 us: shards(): skewed = flat.reshape(groups, span, 2 * span + 1)[:, :, 1:span + 1]]
  transfers between devices with their start and end apart: 7 -> 0, of which waited for: 5 -> 0; matrix products, arithmetic and copies ran while one was open for 15% -> 0% of each run, Pallas kernels for 0% -> 0%
where the time goes in v1:
time: 146 us; the launch traced here: 145 us
  Pallas kernels  136 us (93%)
  local copies, waits for them, and re-layouts  7.75 us (5%)
    pallas_call x1, Pallas kernels, shards(): pl.pallas_call(kernel, out_shape=(act, act, act, act, jax.ShapeDtypeStruc...  136 us
    unnamed x13, local copies, waits for them, and re-layouts  4.96 us

profile of v1, /device:TPU:1, one launch (start us, length us, event | category | flops | bytes accessed | tf_op | source)
XLA Modules:
  0.0 144.7 jit_solution(8354386930039553929)
XLA Ops:
  0.6 1.4 rev.6.fr_ref
  2.0 136.3 %shard_map.109 = (bf16[256,512]{1,0:T(8,128)(2,1)}, bf16[256,512]{1,0:T(8,128)(2,1)}, bf16[256,512]{1,0:T(8,128)(2,1)}, bf16[256,512]{1,0:T(8,128)(2,1)}, bf16[512,512]{1,0:T(8,128)(2,1)}, /*index=5*/f32[32,128]{1,0:T(8,128)}) custom-call(bf16[256,512]{1,0:T(8,128)(2,1)} %q_ref.1, bf16[256,512]{1,0:T(8,128)(2,1)} %k_ref.1, bf16[256,512]{1,0:T(8,128)(2,1)} %v_ref.1, ...), custom_call_target="tpu_custom_call" | custom-call | tf_op jit(solution)/shard_map/pallas_call | solution.py:445
  138.3 1.4 rev.7
  139.7 0.0 copy-start.3
  139.7 1.7 %copy.17 = bf16[256,512]{1,0:T(8,128)(2,1)} copy(bf16[256,512]{1,0:T(8,128)(2,1)} %get-tuple-element.24) | data formatting | bytes 524288
  141.4 0.0 copy-done.3
  141.4 0.0 copy-start.2
  141.4 0.0 copy-start.1
  141.4 0.7 copy.18
  142.1 0.3 copy-done.2
  142.5 0.0 copy-start
  142.5 0.7 copy.19
  143.2 0.0 copy-done.1
  143.2 0.7 copy.20
  143.9 0.0 copy-done
  143.9 0.8 copy.21
Async XLA Ops:
  139.7 1.7 %copy-start.3 = (bf16[256,512]{1,0:T(8,128)(2,1)S(1)}, bf16[256,512]{1,0:T(8,128)(2,1)}, u32[]{:S(2)}) copy-start(bf16[256,512]{1,0:T(8,128)(2,1)} %get-tuple-element.25) | copy-start | bytes 786436
  141.4 1.0 copy-start.2
  141.4 1.8 %copy-start.1 = (bf16[256,512]{1,0:T(8,128)(2,1)S(1)}, bf16[256,512]{1,0:T(8,128)(2,1)}, u32[]{:S(2)}) copy-start(bf16[256,512]{1,0:T(8,128)(2,1)} %get-tuple-element.27) | copy-start | bytes 786436
  142.5 1.4 copy-start

commit v2 on v1

v2 whole, which is shorter than its diff:
```python
import math

import jax
import jax.numpy as jnp
from jax import lax
from jax.experimental import pallas as pl
from jax.experimental.pallas import tpu as pltpu
from jax.sharding import PartitionSpec as P

F32 = jnp.float32
BF16 = jnp.bfloat16
MESH = pl.DeviceIdType.MESH
NT = (((1,), (1,)), ((), ()))
TN = (((0,), (0,)), ((), ()))
NN = (((1,), (0,)), ((), ()))


def dot(a, b, dims=NN):
    return lax.dot_general(a, b, dims, preferred_element_type=F32)


def split(x):
    high = x.astype(BF16)
    return high, (x - high.astype(F32)).astype(BF16)


def kernel(
    q_ref, k_ref, v_ref, f_ref, w_ref, og_ref,
    mixed_ref, qg_ref, kg_ref, vg_ref, wg_ref, fg_ref,
    k_rim, v_rim, g_rim, back,
    t_hi, t_lo, a_hi, a_lo, x_hi, x_lo, conv, gc,
    wp, gp, pb, rp, py, pair, wb, sb, xfar, xnear, yb,
    taps, tin, acc, ss, rs, ls,
):
    tok, wid = q_ref.shape
    span = f_ref.shape[1]
    groups = f_ref.shape[0]
    group = wid // groups
    lanes = 128
    tiles = wid // lanes
    per = lanes // group
    half = tok // 2
    whalf = wid // 2

    r = lax.axis_index("row")
    c = lax.axis_index("col")
    x, yh, core = r // 4, lax.rem(r // 2, 2), lax.rem(r, 2)
    yl, z = c // 8, lax.rem(c, 8)

    def rowid(dx, flip_y, flip_core):
        yy = 1 - yh if flip_y else yh
        cc = 1 - core if flip_core else core
        return lax.rem(x + dx + 4, 4) * 4 + yy * 2 + cc

    def colid(dz, flip_y):
        yy = 1 - yl if flip_y else yl
        return yy * 8 + lax.rem(z + dz + 8, 8)

    sib = (rowid(0, 0, 1), c)
    ytwo = (rowid(0, 1, 0), c)
    ysib = (rowid(0, 1, 1), c)
    xdev = {d: (rowid(d, 0, 0), c) for d in (1, -1, 2)}
    zdev = {1: (r, colid(1, 0)), -1: (r, colid(-1, 0))}
    ypair = (r, colid(0, 1))
    after = (lax.rem(r + 1, 16), c)
    before = (lax.rem(r + 15, 16), c)

    barrier = pltpu.get_barrier_semaphore()
    peers = [sib, ytwo, ysib, xdev[1], xdev[-1], xdev[2]]
    peers += [zdev[1], zdev[-1], ypair, after, before]
    for peer in peers:
        pl.semaphore_signal(barrier, inc=1, device_id=peer, device_id_type=MESH)
    pl.semaphore_wait(barrier, len(peers))

    names = {}
    started = []

    def slot(name):
        return names.setdefault(name, len(names))

    def desc(src, dst, name, dev):
        n = name if not isinstance(name, str) else slot(name)
        return pltpu.make_async_remote_copy(
            src_ref=src, dst_ref=dst, send_sem=ss.at[n], recv_sem=rs.at[n],
            device_id=dev, device_id_type=MESH,
        )

    def send(src, dst, name, dev):
        copy = desc(src, dst, name, dev)
        copy.start()
        started.append(copy)

    def recv(dst, name, dev):
        desc(dst, dst, name, dev).wait_recv()

    def add_into(dst, src):
        step = 64

        def body(i, carry):
            rows = pl.ds(pl.multiple_of(i * step, step), step)
            dst[rows, :] = (dst[rows, :].astype(F32) + src[rows, :].astype(F32)).astype(BF16)
            return carry

        lax.fori_loop(0, dst.shape[0] // step, body, 0)

    send(k_ref.at[pl.ds(tok - span, span)], k_rim, "hk", after)
    send(v_ref.at[pl.ds(tok - span, span)], v_rim, "hv", after)

    def far_half(s):
        return 0 if s == 1 else 1

    def wh(blk, h):
        return wp.at[blk, pl.ds(h * whalf, whalf)]

    for h in (0, 1):
        part = w_ref.at[pl.ds(h * whalf, whalf)]
        send(part, wh(r, h), f"w_y_{h}", ytwo)
    for k in (0, 1):
        for s in (1, -1):
            h = far_half(s) if k == 0 else 1 - far_half(s)
            part = w_ref.at[pl.ds(h * whalf, whalf)]
            send(part, wh(r, h), f"w_x{s}0_{h}", xdev[s])
    send(w_ref, wp.at[r], "w_s00", sib)
    own = pltpu.make_async_copy(w_ref, wp.at[r], ls.at[0])
    own.start()

    flip_taps = (
        lax.broadcasted_iota(jnp.int32, (span, span), 0)
        + lax.broadcasted_iota(jnp.int32, (span, span), 1)
    ) == span - 1
    flip_taps = jnp.where(flip_taps, 1.0, 0.0).astype(BF16)

    def reversed_taps(value):
        high, low = split(value)
        rest = (value - high.astype(F32) - low.astype(F32)).astype(BF16)
        return dot(high, flip_taps) + dot(low, flip_taps) + dot(rest, flip_taps)

    def shear(row, shift):
        wide = jnp.concatenate([row, jnp.zeros((1, span), F32)], axis=1)
        wide = jnp.broadcast_to(wide, (span, 2 * span))
        return pltpu.roll(wide, shift, 1, stride=1, stride_axis=0)

    def build(source, high_ref, low_ref, shift):
        def body(g, carry):
            rows = pl.ds(pl.multiple_of(g * span, span), span)
            high, low = split(shear(source[pl.ds(g, 1), :], shift))
            high_ref[rows, :] = high
            low_ref[rows, :] = low
            return carry

        lax.fori_loop(0, groups, body, 0)

    lane_group = lax.broadcasted_iota(jnp.int32, (span, 2 * lanes), 1)
    lane_group = lax.rem(lane_group, lanes) // group

    def pick(full):
        out = full[0:span]
        for g in range(1, per):
            out = jnp.where(lane_group == g, full[g * span:(g + 1) * span], out)
        return out

    def two(ref, cols):
        return jnp.concatenate(
            [ref[pl.ds(0, 2 * span), cols], ref[pl.ds(span, 2 * span), cols]], axis=1
        )

    back[...] = reversed_taps(f_ref[...])
    build(back, t_hi, t_lo, 1)
    high, low = split(k_ref[...].astype(F32) * v_ref[...].astype(F32))
    x_hi[pl.ds(span, tok), :] = high
    x_lo[pl.ds(span, tok), :] = low
    recv(k_rim, "hk", before)
    recv(v_rim, "hv", before)
    rim = k_rim[...].astype(F32) * v_rim[...].astype(F32)
    high, low = split(jnp.where(r > 0, rim, 0.0))
    x_hi[pl.ds(0, span), :] = high
    x_lo[pl.ds(0, span), :] = low

    def forward(j, carry):
        cols = pl.ds(pl.multiple_of(j * lanes, lanes), lanes)
        taps_rows = pl.ds(pl.multiple_of(j * per * span, per * span), per * span)
        mh = t_hi[taps_rows, :]
        xh = two(x_hi, cols)
        out = pick(dot(mh, xh) + dot(mh, two(x_lo, cols)) + dot(t_lo[taps_rows, :], xh))
        for b in range(2):
            rows = pl.ds(b * span, span)
            part = out[:, b * lanes:(b + 1) * lanes]
            conv[rows, cols] = part
            gp[c, rows, cols] = (q_ref[rows, cols].astype(F32) * part).astype(BF16)
        return carry

    every = pl.ds(0, tok)

    def gh(blk, h):
        return gp.at[blk, every, pl.ds(h * whalf, whalf)]

    for h in (0, 1):
        lax.fori_loop(h * tiles // 2, (h + 1) * tiles // 2, forward, 0)
        send(gh(c, h), gh(c, h), f"gy_0{h}", ypair)
        for s in (1, -1):
            send(gh(c, h), gh(c, h), f"g_{s}_0_1_{h}", zdev[s])

    def g_step(flip, dist):
        for h in (0, 1):
            for s in (1, -1):
                blk = colid(-s * dist, flip)
                if dist == 4:
                    if h == far_half(s):
                        recv(gh(blk, h), f"g_{s}_{flip}_4_{h}", zdev[-s])
                    continue
                recv(gh(blk, h), f"g_{s}_{flip}_{dist}_{h}", zdev[-s])
                onward = dist < 2 if flip else dist < 3 or h == far_half(s)
                if onward:
                    send(gh(blk, h), gh(blk, h), f"g_{s}_{flip}_{dist + 1}_{h}", zdev[s])
        if not flip and dist > 2:
            for d in (-3, 3) if dist == 3 else (4,):
                blk = colid(d, 0)
                send(gp.at[blk], gp.at[blk], f"gy_{d}", ypair)

    def w_far(flip):
        for s in (1, -1):
            blk, h = rowid(-s, flip, 0), far_half(s)
            recv(wh(blk, h), f"w_x{s}{flip}_{h}", xdev[-s])
            send(wh(blk, h), wh(blk, h), f"w_far{s}{flip}", xdev[s])

    def w_near(flip):
        for s in (1, -1):
            blk, h = rowid(-s, flip, 0), 1 - far_half(s)
            recv(wh(blk, h), f"w_x{s}{flip}_{h}", xdev[-s])
            send(wp.at[blk], wp.at[blk], f"w_s{s}{flip}", sib)

    def w_two():
        blk = rowid(0, 1, 0)
        for h in (0, 1):
            recv(wh(blk, h), f"w_y_{h}", ytwo)
        for k in (0, 1):
            for s in (1, -1):
                h = far_half(s) if k == 0 else 1 - far_half(s)
                send(wh(blk, h), wh(blk, h), f"w_x{s}1_{h}", xdev[s])
        send(wp.at[blk], wp.at[blk], "w_s01", sib)

    def w_last(flip):
        blk = rowid(2, flip, 0)
        for s in (1, -1):
            h = far_half(s)
            recv(wh(blk, h), f"w_far{s}{flip}", xdev[-s])
            send(wh(blk, h), wh(blk, h), f"w_s2{flip}_{h}", sib)

    def g_partner():
        blk = colid(0, 1)
        for h in (0, 1):
            recv(gh(blk, h), f"gy_0{h}", ypair)
            for s in (1, -1):
                send(gh(blk, h), gh(blk, h), f"g_{s}_1_1_{h}", zdev[s])

    w_far(0)
    g_step(0, 1)
    w_two()
    w_near(0)
    g_step(0, 2)
    g_partner()
    w_last(0)
    build(f_ref, a_hi, a_lo, 0)
    w_far(1)
    g_step(0, 3)
    g_step(1, 1)
    w_near(1)
    g_step(0, 4)
    w_last(1)
    own.wait()
    for flip in (0, 1):
        recv(wp.at[rowid(0, flip, 1)], f"w_s0{flip}", sib)
        for d in (1, -1):
            recv(wp.at[rowid(-d, flip, 1)], f"w_s{d}{flip}", sib)
        for h in (0, 1):
            recv(wh(rowid(2, flip, 1), h), f"w_s2{flip}_{h}", sib)

    def partial(i, carry):
        dest = lax.rem(1 - yl + i // 8, 2) * 8 + lax.rem(z + i, 8)
        pb[dest] = dot(og_ref[...], wp[dest], NT).astype(BF16)
        return carry

    def hrows(h):
        return pl.ds(h * half, half)

    def p_pass(flip, dist):
        far = 2 if flip else 4
        for h in (0, 1):
            for n, s in enumerate((1, -1)):
                hh = 1 - h if s == 1 else h
                rows = hrows(hh)
                dest = colid(s * dist, flip)
                if dist == 4 and hh != far_half(s):
                    continue
                if dist < far and not (dist == 3 and hh != far_half(s)):
                    recv(rp.at[n, flip, dist, rows], f"p_{s}_{flip}_{dist + 1}_{hh}", zdev[-s])
                    add_into(pb.at[dest, rows], rp.at[n, flip, dist, rows])
                send(
                    pb.at[dest, rows], rp.at[n, flip, dist - 1, rows],
                    f"p_{s}_{flip}_{dist}_{hh}", zdev[s],
                )

    lax.fori_loop(2, 7, partial, 0)
    for n, d in enumerate((4, 3, -3)):
        send(pb.at[colid(d, 1)], py.at[n], f"py_{d}", ypair)
    p_pass(1, 2)
    lax.fori_loop(7, 16, partial, 0)
    lax.fori_loop(0, 2, partial, 0)
    recv(py.at[0], "py_4", ypair)
    add_into(pb.at[colid(4, 0)], py.at[0])
    p_pass(0, 4)
    g_step(1, 2)
    for n, d in ((1, 3), (2, -3)):
        recv(py.at[n], f"py_{d}", ypair)
        add_into(pb.at[colid(d, 0)], py.at[n])
    p_pass(1, 1)
    p_pass(0, 3)
    for d in (-3, 3, 4):
        recv(gp.at[colid(d, 1)], f"gy_{d}", ypair)

    sib_base = slot("s_0")
    for i in range(1, 8):
        slot(f"s_{i}")

    def order_row(i, cc):
        dx = jnp.where(i < 2, 2, jnp.where(i >= 6, 0, jnp.where(lax.rem(i, 2) == 0, 1, 3)))
        flip = jnp.where(i < 2, 1 - i, jnp.where(i >= 6, 7 - i, jnp.where(i < 4, 1, 0)))
        yy = lax.rem(yh + flip, 2)
        return lax.rem(x + dx, 4) * 4 + yy * 2 + cc

    def for_sib(i, carry):
        dest = order_row(i, 1 - core)
        wb[dest] = dot(gp[dest], og_ref[...], TN).astype(BF16)
        desc(wb.at[dest], sb.at[i], sib_base + i, sib).start()
        return carry

    def for_own(i, carry):
        dest = order_row(i, core)
        part = dot(gp[dest], og_ref[...], TN)
        desc(sb.at[i], sb.at[i], sib_base + i, sib).wait_recv()
        wb[dest] = (part + sb[i].astype(F32)).astype(BF16)
        return carry

    def w_half(s):
        return pl.ds(0 if s == 1 else whalf, whalf)

    def wx_far(flip):
        for n, s in enumerate((1, -1)):
            dest = rowid(2, flip, 0)
            rows = w_half(s)
            send(wb.at[dest, rows], xfar.at[n, flip], f"x_far{s}_{flip}", xdev[s])

    def wx_near(flip):
        for n, s in enumerate((1, -1)):
            dest = rowid(s, flip, 0)
            rows = w_half(s)
            recv(xfar.at[n, flip], f"x_far{s}_{flip}", xdev[-s])
            add_into(wb.at[dest, rows], xfar.at[n, flip])
            send(wb.at[dest], xnear.at[n, flip], f"x_near{s}_{flip}", xdev[s])

    lax.fori_loop(0, 4, for_sib, 0)
    lax.fori_loop(0, 2, for_own, 0)
    wx_far(1)
    wx_far(0)
    lax.fori_loop(4, 8, for_sib, 0)
    p_pass(0, 2)
    lax.fori_loop(2, 8, for_own, 0)
    wx_near(1)
    wx_near(0)

    blk = colid(0, 1)
    for h in (0, 1):
        rows = hrows(h)
        for n, s in enumerate((1, -1)):
            recv(rp.at[n, 1, 0, rows], f"p_{s}_1_1_{h}", zdev[-s])
            add_into(pb.at[blk, rows], rp.at[n, 1, 0, rows])
    send(pb.at[blk], pair, "py_0", ypair)
    p_pass(0, 1)

    acc[...] = jnp.zeros_like(acc)

    def mix(i, carry):
        acc[...] += dot(gp[i], wp[i])
        return carry

    lax.fori_loop(0, 16, mix, 0)
    mixed_ref[...] = acc[...].astype(BF16)

    def w_total(flip):
        dest = rowid(0, flip, 0)
        for n, s in enumerate((1, -1)):
            recv(xnear.at[n, flip], f"x_near{s}_{flip}", xdev[-s])
            add_into(wb.at[dest], xnear.at[n, flip])

    w_total(1)
    send(wb.at[rowid(0, 1, 0)], yb, "x_y", ytwo)

    recv(pair, "py_0", ypair)
    step = 64

    def gradients(i, carry):
        rows = pl.ds(pl.multiple_of(i * step, step), step)
        total = pb[c, rows, :].astype(F32) + rp[0, 0, 0, rows, :].astype(F32)
        total += rp[1, 0, 0, rows, :].astype(F32) + pair[rows, :].astype(F32)
        qg_ref[rows, :] = (total * conv[rows, :]).astype(BF16)
        gc[rows, :] = (total * q_ref[rows, :].astype(F32)).astype(BF16)
        return carry

    for h in (0, 1):
        for n, s in enumerate((1, -1)):
            recv(rp.at[n, 0, 0, hrows(h)], f"p_{s}_0_1_{h}", zdev[-s])
        lax.fori_loop(h * half // step, (h + 1) * half // step, gradients, 0)
        if h == 0:
            send(gc.at[pl.ds(0, span)], g_rim, "rim", before)

    def corr(j, carry):
        cols = pl.ds(pl.multiple_of(j * lanes, lanes), lanes)
        grad = jnp.concatenate([gc[pl.ds(0, span), cols], gc[pl.ds(span, span), cols]], axis=1)
        grad = grad.astype(F32)
        masked = jnp.concatenate(
            [jnp.where(lane_group == g, grad, 0.0).astype(BF16) for g in range(per)], axis=0
        )
        full = dot(masked, two(x_hi, cols), NT) + dot(masked, two(x_lo, cols), NT)
        for g in range(per):
            block = full[g * span:(g + 1) * span]
            size = span
            while size > 8:
                size //= 2
                block = block[0:size] + pltpu.roll(block[size:2 * size], 2 * span - size, 1)
            sub = lax.broadcasted_iota(jnp.int32, (8, 2 * span), 0)
            for bit in (4, 2, 1):
                moved = pltpu.roll(block, 2 * span - bit, 1)
                block = jnp.where((sub // bit) % 2 == 1, moved, block)
            line = jnp.sum(block, axis=0, keepdims=True)
            taps[pl.ds(j * per + g, 1), :] = line
        return carry

    lax.fori_loop(0, tiles, corr, 0)
    tin[x] = taps[...][:, 1:span + 1]
    for d in (1, -1, 2):
        send(tin.at[x], tin.at[x], f"t_{d}", xdev[d])

    def backward(j, carry):
        cols = pl.ds(pl.multiple_of(j * lanes, lanes), lanes)
        taps_rows = pl.ds(pl.multiple_of(j * per * span, per * span), per * span)
        rimv = jnp.where(r < 15, g_rim[:, cols].astype(F32), 0.0).astype(BF16)
        lower = gc[pl.ds(0, span), cols]
        upper = gc[pl.ds(span, span), cols]
        ext = jnp.concatenate(
            [jnp.concatenate([lower, upper], axis=0), jnp.concatenate([upper, rimv], axis=0)],
            axis=1,
        )
        out = pick(dot(a_hi[taps_rows, :], ext) + dot(a_lo[taps_rows, :], ext))
        for b in range(2):
            rows = pl.ds(b * span, span)
            part = out[:, b * lanes:(b + 1) * lanes]
            kg_ref[rows, cols] = (part * v_ref[rows, cols].astype(F32)).astype(BF16)
            vg_ref[rows, cols] = (part * k_ref[rows, cols].astype(F32)).astype(BF16)
        return carry

    recv(g_rim, "rim", after)
    lax.fori_loop(0, tiles // 2, backward, 0)
    for d in (1, -1, 2):
        recv(tin.at[rowid(-d, 0, 0) // 4], f"t_{d}", xdev[-d if d != 2 else 2])
    quad = yh * 2 + core
    tin[4 + quad] = (tin[0] + tin[1]) + (tin[2] + tin[3])
    mates = ((sib, yh * 2 + 1 - core), (ytwo, 2 - 2 * yh + core), (ysib, 3 - quad))
    for n, (dev, _) in enumerate(mates):
        send(tin.at[4 + quad], tin.at[4 + quad], f"t_q{n}", dev)
    lax.fori_loop(tiles // 2, tiles, backward, 0)

    w_total(0)
    for n, (dev, place) in enumerate(mates):
        recv(tin.at[4 + place], f"t_q{n}", dev)
    total = (tin[4] + tin[5]) + (tin[6] + tin[7])
    fg_ref[...] = reversed_taps(total * (1.0 / math.sqrt(tok * 16 * group)))

    recv(yb, "x_y", ytwo)
    final = wb.at[r]
    scale = 1.0 / math.sqrt(tok * 16)

    def finish(i, carry):
        rows = pl.ds(pl.multiple_of(i * step, step), step)
        wg_ref[rows, :] = (
            (final[rows, :].astype(F32) + yb[rows, :].astype(F32)) * scale
        ).astype(BF16)
        return carry

    lax.fori_loop(0, wid // step, finish, 0)

    for copy in started:
        copy.wait_send()

    def drain(i, carry):
        desc(wb.at[0], sb.at[i], sib_base + i, sib).wait_send()
        return carry

    lax.fori_loop(0, 8, drain, 0)
    assert len(names) <= ss.shape[0], len(names)


def relay(*refs):
    ins, outs, bufs, sems = refs[0:6], refs[6:12], refs[12:18], refs[18]
    first = [pltpu.make_async_copy(a, b, sems.at[0, n]) for n, (a, b) in enumerate(zip(ins, bufs))]
    second = [pltpu.make_async_copy(a, b, sems.at[1, n]) for n, (a, b) in enumerate(zip(bufs, outs))]
    for copy in first:
        copy.start()
    for n in range(6):
        first[n].wait()
        second[n].start()
    for copy in second:
        copy.wait()


def shards(query_in, key_in, value_in, filters, out_weight, out_grad):
    tok, wid = query_in.shape
    groups, span = filters.shape
    act = jax.ShapeDtypeStruct((tok, wid), BF16)
    vmem = pl.BlockSpec(memory_space=pltpu.VMEM)
    sems = 120
    shapes = (
        act, act, act, act,
        jax.ShapeDtypeStruct((wid, wid), BF16),
        jax.ShapeDtypeStruct((groups, span), F32),
    )
    results = pl.pallas_call(
        kernel,
        out_shape=shapes,
        in_specs=[vmem] * 6,
        out_specs=[vmem] * 6,
        scratch_shapes=[
            pltpu.VMEM((span, wid), BF16),
            pltpu.VMEM((span, wid), BF16),
            pltpu.VMEM((span, wid), BF16),
            pltpu.VMEM((groups, span), F32),
            pltpu.VMEM((groups * span, 2 * span), BF16),
            pltpu.VMEM((groups * span, 2 * span), BF16),
            pltpu.VMEM((groups * span, 2 * span), BF16),
            pltpu.VMEM((groups * span, 2 * span), BF16),
            pltpu.VMEM((span + tok, wid), BF16),
            pltpu.VMEM((span + tok, wid), BF16),
            pltpu.VMEM((tok, wid), F32),
            pltpu.VMEM((tok, wid), BF16),
            pltpu.VMEM((16, wid, wid), BF16),
            pltpu.VMEM((16, tok, wid), BF16),
            pltpu.VMEM((16, tok, wid), BF16),
            pltpu.VMEM((2, 2, 4, tok, wid), BF16),
            pltpu.VMEM((3, tok, wid), BF16),
            pltpu.VMEM((tok, wid), BF16),
            pltpu.VMEM((16, wid, wid), BF16),
            pltpu.VMEM((8, wid, wid), BF16),
            pltpu.VMEM((2, 2, wid // 2, wid), BF16),
            pltpu.VMEM((2, 2, wid, wid), BF16),
            pltpu.VMEM((wid, wid), BF16),
            pltpu.VMEM((groups, 2 * span), F32),
            pltpu.VMEM((8, groups, span), F32),
            pltpu.VMEM((tok, wid), F32),
            pltpu.SemaphoreType.DMA((sems,)),
            pltpu.SemaphoreType.DMA((sems,)),
            pltpu.SemaphoreType.DMA((1,)),
        ],
        compiler_params=pltpu.CompilerParams(
            collective_id=0, has_side_effects=True, vmem_limit_bytes=67_000_000
        ),
    )(query_in, key_in, value_in, filters, out_weight, out_grad)
    anywhere = pl.BlockSpec(memory_space=pl.ANY)
    return pl.pallas_call(
        relay,
        out_shape=shapes,
        in_specs=[anywhere] * 6,
        out_specs=[anywhere] * 6,
        scratch_shapes=[pltpu.VMEM(a.shape, a.dtype) for a in shapes]
        + [pltpu.SemaphoreType.DMA((2, 6))],
    )(*results)


def solution(mesh):
    placed = (
        P("row", "col"),
        P("row", "col"),
        P("row", "col"),
        P("col", None),
        P("row", "col"),
        P("row", "col"),
    )
    return jax.shard_map(
        shards,
        mesh=mesh,
        in_specs=placed,
        out_specs=(
            P("row", "col"),
            P("row", "col"),
            P("row", "col"),
            P("row", "col"),
            P("row", "col"),
            P("col", None),
        ),
        check_vma=False,
    )
```

time: 146 us -> 129 us (0.88); the launches traced: 145 us -> 129 us
  local copies, waits for them, and re-layouts: 7.75 us -> 0 us
  Pallas kernels: 136 us -> 129 us
    pallas_call x1 -> x2, Pallas kernels: 136 us -> 129 us  [the longest x1 126 us: shards(): pl.pallas_call(kernel, out_shape=shapes, in_specs=[vmem] * 6, out_specs=[...]
    unnamed x13 -> x0, local copies, waits for them, and re-layouts: 4.96 us -> none
    rev x2 -> x0, local copies, waits for them, and re-layouts: 2.79 us -> none  [the longest x1 1.4 us: shards(): return (mixed, qg, kg, vg, wg, fg[:, ::-1])]
where the time goes in v2:
time: 129 us
  Pallas kernels  129 us (100%)
    pallas_call x1, Pallas kernels, shards(): pl.pallas_call(kernel, out_shape=shapes, in_specs=[vmem] * 6, out_specs=[...  126 us

profile of v2, /device:TPU:1, one launch (start us, length us, event | category | flops | bytes accessed | tf_op | source)
XLA Modules:
  0.0 129.4 jit_solution(17298336466619860772)
XLA Ops:
  0.6 126.5 %shard_map.109 = (bf16[256,512]{1,0:T(8,128)(2,1)}, bf16[256,512]{1,0:T(8,128)(2,1)}, bf16[256,512]{1,0:T(8,128)(2,1)}, bf16[256,512]{1,0:T(8,128)(2,1)}, bf16[512,512]{1,0:T(8,128)(2,1)}, /*index=5*/f32[32,128]{1,0:T(8,128)}) custom-call(bf16[256,512]{1,0:T(8,128)(2,1)} %q_ref.1, bf16[256,512]{1,0:T(8,128)(2,1)} %k_ref.1, bf16[256,512]{1,0:T(8,128)(2,1)} %v_ref.1, ...), custom_call_target="tpu_custom_call" | custom-call | tf_op jit(solution)/shard_map/pallas_call | solution.py:526
  127.1 2.3 %shard_map.110 = (bf16[256,512]{1,0:T(8,128)(2,1)}, bf16[256,512]{1,0:T(8,128)(2,1)}, bf16[256,512]{1,0:T(8,128)(2,1)}, bf16[256,512]{1,0:T(8,128)(2,1)}, bf16[512,512]{1,0:T(8,128)(2,1)}, /*index=5*/f32[32,128]{1,0:T(8,128)}) custom-call(bf16[256,512]{1,0:T(8,128)(2,1)} %get-tuple-element.12.refs_0_, bf16[256,512]{1,0:T(8,128)(2,1)} %get-tuple-element.13.refs_1_, ...), custom_call_target="tpu_custom_call" | custom-call | tf_op jit(solution)/shard_map/pallas_call | solution.py:567

commit v3 on v2

--- a/solution.py
+++ b/solution.py
@@ -135,28 +135,32 @@
         rest = (value - high.astype(F32) - low.astype(F32)).astype(BF16)
         return dot(high, flip_taps) + dot(low, flip_taps) + dot(rest, flip_taps)
 
-    def shear(row, shift):
-        wide = jnp.concatenate([row, jnp.zeros((1, span), F32)], axis=1)
-        wide = jnp.broadcast_to(wide, (span, 2 * span))
-        return pltpu.roll(wide, shift, 1, stride=1, stride_axis=0)
+    turn = lax.broadcasted_iota(jnp.int32, (span, span), 1)
+    turn = turn - lax.broadcasted_iota(jnp.int32, (span, span), 0)
 
     def build(source, high_ref, low_ref, shift):
+        left = turn >= shift
+
         def body(g, carry):
             rows = pl.ds(pl.multiple_of(g * span, span), span)
-            high, low = split(shear(source[pl.ds(g, 1), :], shift))
-            high_ref[rows, :] = high
-            low_ref[rows, :] = low
+            line = jnp.broadcast_to(source[pl.ds(g, 1), :], (span, span))
+            wide = pltpu.roll(line, shift, 1, stride=1, stride_axis=0)
+            high = wide.astype(BF16).astype(F32)
+            for ref, value in ((high_ref, high), (low_ref, wide - high)):
+                ref[rows, pl.ds(0, span)] = jnp.where(left, value, 0.0).astype(BF16)
+                ref[rows, pl.ds(span, span)] = jnp.where(left, 0.0, value).astype(BF16)
             return carry
 
-        lax.fori_loop(0, groups, body, 0)
+        lax.fori_loop(0, groups, body, 0, unroll=2)
 
     lane_group = lax.broadcasted_iota(jnp.int32, (span, 2 * lanes), 1)
     lane_group = lax.rem(lane_group, lanes) // group
 
     def pick(full):
+        mine = lane_group[:, 0:full.shape[1]]
         out = full[0:span]
         for g in range(1, per):
-            out = jnp.where(lane_group == g, full[g * span:(g + 1) * span], out)
+            out = jnp.where(mine == g, full[g * span:(g + 1) * span], out)
         return out
 
     def two(ref, cols):
@@ -169,39 +173,41 @@
     high, low = split(k_ref[...].astype(F32) * v_ref[...].astype(F32))
     x_hi[pl.ds(span, tok), :] = high
     x_lo[pl.ds(span, tok), :] = low
-    recv(k_rim, "hk", before)
-    recv(v_rim, "hv", before)
-    rim = k_rim[...].astype(F32) * v_rim[...].astype(F32)
-    high, low = split(jnp.where(r > 0, rim, 0.0))
-    x_hi[pl.ds(0, span), :] = high
-    x_lo[pl.ds(0, span), :] = low
-
-    def forward(j, carry):
-        cols = pl.ds(pl.multiple_of(j * lanes, lanes), lanes)
-        taps_rows = pl.ds(pl.multiple_of(j * per * span, per * span), per * span)
-        mh = t_hi[taps_rows, :]
-        xh = two(x_hi, cols)
-        out = pick(dot(mh, xh) + dot(mh, two(x_lo, cols)) + dot(t_lo[taps_rows, :], xh))
-        for b in range(2):
-            rows = pl.ds(b * span, span)
-            part = out[:, b * lanes:(b + 1) * lanes]
+    def forward(b):
+        rows = pl.ds(b * span, span)
+        window = pl.ds(b * span, 2 * span)
+
+        def body(j, carry):
+            cols = pl.ds(pl.multiple_of(j * lanes, lanes), lanes)
+            taps_rows = pl.ds(pl.multiple_of(j * per * span, per * span), per * span)
+            mh = t_hi[taps_rows, :]
+            xh = x_hi[window, cols]
+            full = dot(mh, xh) + dot(mh, x_lo[window, cols]) + dot(t_lo[taps_rows, :], xh)
+            part = pick(full)
             conv[rows, cols] = part
             gp[c, rows, cols] = (q_ref[rows, cols].astype(F32) * part).astype(BF16)
-        return carry
-
-    every = pl.ds(0, tok)
+            return carry
+
+        lax.fori_loop(0, tiles, body, 0)
 
     def gh(blk, h):
-        return gp.at[blk, every, pl.ds(h * whalf, whalf)]
-
-    for h in (0, 1):
-        lax.fori_loop(h * tiles // 2, (h + 1) * tiles // 2, forward, 0)
-        send(gh(c, h), gh(c, h), f"gy_0{h}", ypair)
+        return gp.at[blk, pl.ds(h * half, half)]
+
+    for h in (1, 0):
+        if h == 0:
+            recv(k_rim, "hk", before)
+            recv(v_rim, "hv", before)
+            rim = k_rim[...].astype(F32) * v_rim[...].astype(F32)
+            high, low = split(jnp.where(r > 0, rim, 0.0))
+            x_hi[pl.ds(0, span), :] = high
+            x_lo[pl.ds(0, span), :] = low
+        forward(h)
         for s in (1, -1):
             send(gh(c, h), gh(c, h), f"g_{s}_0_1_{h}", zdev[s])
+        send(gh(c, h), gh(c, h), f"gy_0{h}", ypair)
 
     def g_step(flip, dist):
-        for h in (0, 1):
+        for h in (1, 0):
             for s in (1, -1):
                 blk = colid(-s * dist, flip)
                 if dist == 4:
@@ -248,7 +254,7 @@
 
     def g_partner():
         blk = colid(0, 1)
-        for h in (0, 1):
+        for h in (1, 0):
             recv(gh(blk, h), f"gy_0{h}", ypair)
             for s in (1, -1):
                 send(gh(blk, h), gh(blk, h), f"g_{s}_1_1_{h}", zdev[s])
@@ -284,7 +290,7 @@
         return pl.ds(h * half, half)
 
     def p_pass(flip, dist):
-        far = 2 if flip else 4
+        far = 3 if flip else 4
         for h in (0, 1):
             for n, s in enumerate((1, -1)):
                 hh = 1 - h if s == 1 else h
@@ -292,7 +298,7 @@
                 dest = colid(s * dist, flip)
                 if dist == 4 and hh != far_half(s):
                     continue
-                if dist < far and not (dist == 3 and hh != far_half(s)):
+                if dist < far and not (not flip and dist == 3 and hh != far_half(s)):
                     recv(rp.at[n, flip, dist, rows], f"p_{s}_{flip}_{dist + 1}_{hh}", zdev[-s])
                     add_into(pb.at[dest, rows], rp.at[n, flip, dist, rows])
                 send(
@@ -300,21 +306,12 @@
                     f"p_{s}_{flip}_{dist}_{hh}", zdev[s],
                 )
 
-    lax.fori_loop(2, 7, partial, 0)
-    for n, d in enumerate((4, 3, -3)):
-        send(pb.at[colid(d, 1)], py.at[n], f"py_{d}", ypair)
-    p_pass(1, 2)
-    lax.fori_loop(7, 16, partial, 0)
-    lax.fori_loop(0, 2, partial, 0)
-    recv(py.at[0], "py_4", ypair)
-    add_into(pb.at[colid(4, 0)], py.at[0])
-    p_pass(0, 4)
+    lax.fori_loop(3, 6, partial, 0)
+    send(pb.at[colid(4, 1)], py, "py_4", ypair)
+    p_pass(1, 3)
+    lax.fori_loop(6, 16, partial, 0)
+    lax.fori_loop(0, 3, partial, 0)
     g_step(1, 2)
-    for n, d in ((1, 3), (2, -3)):
-        recv(py.at[n], f"py_{d}", ypair)
-        add_into(pb.at[colid(d, 0)], py.at[n])
-    p_pass(1, 1)
-    p_pass(0, 3)
     for d in (-3, 3, 4):
         recv(gp.at[colid(d, 1)], f"gy_{d}", ypair)
 
@@ -351,49 +348,58 @@
             send(wb.at[dest, rows], xfar.at[n, flip], f"x_far{s}_{flip}", xdev[s])
 
     def wx_near(flip):
+        for late in (0, 1):
+            for n, s in enumerate((1, -1)):
+                dest = rowid(s, flip, 0)
+                h = far_half(s) if late else 1 - far_half(s)
+                rows = pl.ds(h * whalf, whalf)
+                if late:
+                    recv(xfar.at[n, flip], f"x_far{s}_{flip}", xdev[-s])
+                    add_into(wb.at[dest, rows], xfar.at[n, flip])
+                send(wb.at[dest, rows], xnear.at[n, flip, rows], f"x_near{s}_{flip}_{h}", xdev[s])
+
+    def w_total(flip):
+        dest = rowid(0, flip, 0)
         for n, s in enumerate((1, -1)):
-            dest = rowid(s, flip, 0)
-            rows = w_half(s)
-            recv(xfar.at[n, flip], f"x_far{s}_{flip}", xdev[-s])
-            add_into(wb.at[dest, rows], xfar.at[n, flip])
-            send(wb.at[dest], xnear.at[n, flip], f"x_near{s}_{flip}", xdev[s])
+            for h in (0, 1):
+                rows = pl.ds(h * whalf, whalf)
+                recv(xnear.at[n, flip, rows], f"x_near{s}_{flip}_{h}", xdev[-s])
+            add_into(wb.at[dest], xnear.at[n, flip])
+
+    def mix(i, carry):
+        acc[...] += dot(gp[i], wp[i])
+        return carry
 
     lax.fori_loop(0, 4, for_sib, 0)
     lax.fori_loop(0, 2, for_own, 0)
     wx_far(1)
-    wx_far(0)
+    recv(py, "py_4", ypair)
+    add_into(pb.at[colid(4, 0)], py)
+    p_pass(0, 4)
     lax.fori_loop(4, 8, for_sib, 0)
-    p_pass(0, 2)
+    p_pass(1, 2)
     lax.fori_loop(2, 8, for_own, 0)
     wx_near(1)
+    wx_far(0)
+    p_pass(0, 3)
+    acc[...] = jnp.zeros_like(acc)
+    lax.fori_loop(0, 5, mix, 0)
+    p_pass(1, 1)
     wx_near(0)
-
+    lax.fori_loop(5, 10, mix, 0)
+    p_pass(0, 2)
     blk = colid(0, 1)
-    for h in (0, 1):
+    for h in (1, 0):
         rows = hrows(h)
         for n, s in enumerate((1, -1)):
             recv(rp.at[n, 1, 0, rows], f"p_{s}_1_1_{h}", zdev[-s])
             add_into(pb.at[blk, rows], rp.at[n, 1, 0, rows])
     send(pb.at[blk], pair, "py_0", ypair)
-    p_pass(0, 1)
-
-    acc[...] = jnp.zeros_like(acc)
-
-    def mix(i, carry):
-        acc[...] += dot(gp[i], wp[i])
-        return carry
-
-    lax.fori_loop(0, 16, mix, 0)
-    mixed_ref[...] = acc[...].astype(BF16)
-
-    def w_total(flip):
-        dest = rowid(0, flip, 0)
-        for n, s in enumerate((1, -1)):
-            recv(xnear.at[n, flip], f"x_near{s}_{flip}", xdev[-s])
-            add_into(wb.at[dest], xnear.at[n, flip])
-
     w_total(1)
     send(wb.at[rowid(0, 1, 0)], yb, "x_y", ytwo)
+    p_pass(0, 1)
+    lax.fori_loop(10, 16, mix, 0)
+    mixed_ref[...] = acc[...].astype(BF16)
 
     recv(pair, "py_0", ypair)
     step = 64
@@ -545,7 +551,7 @@
             pltpu.VMEM((16, tok, wid), BF16),
             pltpu.VMEM((16, tok, wid), BF16),
             pltpu.VMEM((2, 2, 4, tok, wid), BF16),
-            pltpu.VMEM((3, tok, wid), BF16),
+            pltpu.VMEM((tok, wid), BF16),
             pltpu.VMEM((tok, wid), BF16),
             pltpu.VMEM((16, wid, wid), BF16),
             pltpu.VMEM((8, wid, wid), BF16),

time: 129 us -> 119 us (0.922)
  Pallas kernels: 129 us -> 118 us
    pallas_call x1, Pallas kernels: 126 us -> 116 us  [shards(): pl.pallas_call(kernel, out_shape=shapes, in_specs=[vmem] * 6, out_specs=[...]
where the time goes in v3:
time: 119 us
  Pallas kernels  118 us (99%)
    pallas_call x1, Pallas kernels, shards(): pl.pallas_call(kernel, out_shape=shapes, in_specs=[vmem] * 6, out_specs=[...  116 us

profile of v3, /device:TPU:1, one launch (start us, length us, event | category | flops | bytes accessed | tf_op | source)
XLA Modules:
  0.0 118.7 jit_solution(16971864528141040935)
XLA Ops:
  0.6 115.8 %shard_map.109 = (bf16[256,512]{1,0:T(8,128)(2,1)}, bf16[256,512]{1,0:T(8,128)(2,1)}, bf16[256,512]{1,0:T(8,128)(2,1)}, bf16[256,512]{1,0:T(8,128)(2,1)}, bf16[512,512]{1,0:T(8,128)(2,1)}, /*index=5*/f32[32,128]{1,0:T(8,128)}) custom-call(bf16[256,512]{1,0:T(8,128)(2,1)} %q_ref.1, bf16[256,512]{1,0:T(8,128)(2,1)} %k_ref.1, bf16[256,512]{1,0:T(8,128)(2,1)} %v_ref.1, ...), custom_call_target="tpu_custom_call" | custom-call | tf_op jit(solution)/shard_map/pallas_call | solution.py:532
  116.5 2.3 %shard_map.110 = (bf16[256,512]{1,0:T(8,128)(2,1)}, bf16[256,512]{1,0:T(8,128)(2,1)}, bf16[256,512]{1,0:T(8,128)(2,1)}, bf16[256,512]{1,0:T(8,128)(2,1)}, bf16[512,512]{1,0:T(8,128)(2,1)}, /*index=5*/f32[32,128]{1,0:T(8,128)}) custom-call(bf16[256,512]{1,0:T(8,128)(2,1)} %get-tuple-element.12.refs_0_, bf16[256,512]{1,0:T(8,128)(2,1)} %get-tuple-element.13.refs_1_, ...), custom_call_target="tpu_custom_call" | custom-call | tf_op jit(solution)/shard_map/pallas_call | solution.py:573

commit v4 on v3

--- a/solution.py
+++ b/solution.py
@@ -25,11 +25,13 @@
 
 
 def kernel(
-    q_ref, k_ref, v_ref, f_ref, w_ref, og_ref,
+    q_in, k_in, v_in, f_ref, w_ref, og_in,
+    mixed_out, qg_out, kg_out, vg_out, wg_out, fg_out,
+    q_ref, k_ref, v_ref, og_ref,
     mixed_ref, qg_ref, kg_ref, vg_ref, wg_ref, fg_ref,
     k_rim, v_rim, g_rim, back,
     t_hi, t_lo, a_hi, a_lo, x_hi, x_lo, conv, gc,
-    wp, gp, pb, rp, py, pair, wb, sb, xfar, xnear, yb,
+    wp, gp, pb, rp, py, py3, pair, wb, sb, xfar, xnear, yb,
     taps, tin, acc, ss, rs, ls,
 ):
     tok, wid = q_ref.shape
@@ -58,19 +60,28 @@
 
     sib = (rowid(0, 0, 1), c)
     ytwo = (rowid(0, 1, 0), c)
-    ysib = (rowid(0, 1, 1), c)
-    xdev = {d: (rowid(d, 0, 0), c) for d in (1, -1, 2)}
+    xdev = {d: (rowid(d, 0, 0), c) for d in (1, -1)}
     zdev = {1: (r, colid(1, 0)), -1: (r, colid(-1, 0))}
     ypair = (r, colid(0, 1))
     after = (lax.rem(r + 1, 16), c)
     before = (lax.rem(r + 15, 16), c)
 
     barrier = pltpu.get_barrier_semaphore()
-    peers = [sib, ytwo, ysib, xdev[1], xdev[-1], xdev[2]]
-    peers += [zdev[1], zdev[-1], ypair, after, before]
+    peers = [(lax.rem(r + k, 16), c) for k in range(1, 16)]
+    peers += [zdev[1], zdev[-1], ypair]
     for peer in peers:
         pl.semaphore_signal(barrier, inc=1, device_id=peer, device_id_type=MESH)
-    pl.semaphore_wait(barrier, len(peers))
+
+    def local(src, dst, n):
+        copy = pltpu.make_async_copy(src, dst, ls.at[n])
+        copy.start()
+        return copy
+
+    own = local(w_ref, wp.at[r], 0)
+    k_copy = local(k_in, k_ref, 1)
+    v_copy = local(v_in, v_ref, 2)
+    q_copy = local(q_in, q_ref, 3)
+    og_copy = local(og_in, og_ref, 4)
 
     names = {}
     started = []
@@ -103,26 +114,14 @@
 
         lax.fori_loop(0, dst.shape[0] // step, body, 0)
 
-    send(k_ref.at[pl.ds(tok - span, span)], k_rim, "hk", after)
-    send(v_ref.at[pl.ds(tok - span, span)], v_rim, "hv", after)
-
     def far_half(s):
         return 0 if s == 1 else 1
 
     def wh(blk, h):
         return wp.at[blk, pl.ds(h * whalf, whalf)]
 
-    for h in (0, 1):
-        part = w_ref.at[pl.ds(h * whalf, whalf)]
-        send(part, wh(r, h), f"w_y_{h}", ytwo)
-    for k in (0, 1):
-        for s in (1, -1):
-            h = far_half(s) if k == 0 else 1 - far_half(s)
-            part = w_ref.at[pl.ds(h * whalf, whalf)]
-            send(part, wh(r, h), f"w_x{s}0_{h}", xdev[s])
-    send(w_ref, wp.at[r], "w_s00", sib)
-    own = pltpu.make_async_copy(w_ref, wp.at[r], ls.at[0])
-    own.start()
+    def w_part(h):
+        return w_ref.at[pl.ds(h * whalf, whalf)]
 
     flip_taps = (
         lax.broadcasted_iota(jnp.int32, (span, span), 0)
@@ -170,9 +169,23 @@
 
     back[...] = reversed_taps(f_ref[...])
     build(back, t_hi, t_lo, 1)
+    k_copy.wait()
+    v_copy.wait()
+    q_copy.wait()
+    pl.semaphore_wait(barrier, len(peers))
+
+    send(k_ref.at[pl.ds(tok - span, span)], k_rim, "hk", after)
+    send(v_ref.at[pl.ds(tok - span, span)], v_rim, "hv", after)
+    for k in (0, 1):
+        for s in (1, -1):
+            h = far_half(s) if k == 0 else 1 - far_half(s)
+            send(w_part(h), wh(r, h), f"w_x{s}0_{h}", xdev[s])
+    send(w_ref, wp.at[r], "w_s00", sib)
+
     high, low = split(k_ref[...].astype(F32) * v_ref[...].astype(F32))
     x_hi[pl.ds(span, tok), :] = high
     x_lo[pl.ds(span, tok), :] = low
+
     def forward(b):
         rows = pl.ds(b * span, span)
         window = pl.ds(b * span, 2 * span)
@@ -193,35 +206,17 @@
     def gh(blk, h):
         return gp.at[blk, pl.ds(h * half, half)]
 
-    for h in (1, 0):
-        if h == 0:
-            recv(k_rim, "hk", before)
-            recv(v_rim, "hv", before)
-            rim = k_rim[...].astype(F32) * v_rim[...].astype(F32)
-            high, low = split(jnp.where(r > 0, rim, 0.0))
-            x_hi[pl.ds(0, span), :] = high
-            x_lo[pl.ds(0, span), :] = low
-        forward(h)
-        for s in (1, -1):
-            send(gh(c, h), gh(c, h), f"g_{s}_0_1_{h}", zdev[s])
-        send(gh(c, h), gh(c, h), f"gy_0{h}", ypair)
-
-    def g_step(flip, dist):
-        for h in (1, 0):
-            for s in (1, -1):
-                blk = colid(-s * dist, flip)
-                if dist == 4:
-                    if h == far_half(s):
-                        recv(gh(blk, h), f"g_{s}_{flip}_4_{h}", zdev[-s])
-                    continue
-                recv(gh(blk, h), f"g_{s}_{flip}_{dist}_{h}", zdev[-s])
-                onward = dist < 2 if flip else dist < 3 or h == far_half(s)
-                if onward:
-                    send(gh(blk, h), gh(blk, h), f"g_{s}_{flip}_{dist + 1}_{h}", zdev[s])
-        if not flip and dist > 2:
-            for d in (-3, 3) if dist == 3 else (4,):
-                blk = colid(d, 0)
-                send(gp.at[blk], gp.at[blk], f"gy_{d}", ypair)
+    def g_step(flip, dist, h):
+        for s in (1, -1):
+            blk = colid(-s * dist, flip)
+            if dist == 4 and h != far_half(s):
+                continue
+            recv(gh(blk, h), f"g_{s}_{flip}_{dist}_{h}", zdev[-s])
+            onward = dist < 2 if flip else dist < 3 or (dist == 3 and h == far_half(s))
+            if onward:
+                send(gh(blk, h), gh(blk, h), f"g_{s}_{flip}_{dist + 1}_{h}", zdev[s])
+            if not flip and dist > 2:
+                send(gh(blk, h), gh(blk, h), f"gy_{s * dist if dist == 3 else 4}_{h}", ypair)
 
     def w_far(flip):
         for s in (1, -1):
@@ -235,15 +230,13 @@
             recv(wh(blk, h), f"w_x{s}{flip}_{h}", xdev[-s])
             send(wp.at[blk], wp.at[blk], f"w_s{s}{flip}", sib)
 
-    def w_two():
+    def w_two(h):
         blk = rowid(0, 1, 0)
-        for h in (0, 1):
-            recv(wh(blk, h), f"w_y_{h}", ytwo)
-        for k in (0, 1):
-            for s in (1, -1):
-                h = far_half(s) if k == 0 else 1 - far_half(s)
-                send(wh(blk, h), wh(blk, h), f"w_x{s}1_{h}", xdev[s])
-        send(wp.at[blk], wp.at[blk], "w_s01", sib)
+        recv(wh(blk, h), f"w_y_{h}", ytwo)
+        for s in (1, -1):
+            send(wh(blk, h), wh(blk, h), f"w_x{s}1_{h}", xdev[s])
+        if h == 1:
+            send(wp.at[blk], wp.at[blk], "w_s01", sib)
 
     def w_last(flip):
         blk = rowid(2, flip, 0)
@@ -252,28 +245,52 @@
             recv(wh(blk, h), f"w_far{s}{flip}", xdev[-s])
             send(wh(blk, h), wh(blk, h), f"w_s2{flip}_{h}", sib)
 
-    def g_partner():
+    def g_partner(h):
         blk = colid(0, 1)
-        for h in (1, 0):
-            recv(gh(blk, h), f"gy_0{h}", ypair)
-            for s in (1, -1):
-                send(gh(blk, h), gh(blk, h), f"g_{s}_1_1_{h}", zdev[s])
-
+        recv(gh(blk, h), f"gy_0{h}", ypair)
+        for s in (1, -1):
+            send(gh(blk, h), gh(blk, h), f"g_{s}_1_1_{h}", zdev[s])
+
+    def g_own(h):
+        forward(h)
+        for s in (1, -1):
+            send(gh(c, h), gh(c, h), f"g_{s}_0_1_{h}", zdev[s])
+
+    g_own(1)
+    for h in (0, 1):
+        send(w_part(h), wh(r, h), f"w_y_{h}", ytwo)
+    recv(k_rim, "hk", before)
+    recv(v_rim, "hv", before)
+    rim = k_rim[...].astype(F32) * v_rim[...].astype(F32)
+    high, low = split(jnp.where(r > 0, rim, 0.0))
+    x_hi[pl.ds(0, span), :] = high
+    x_lo[pl.ds(0, span), :] = low
+    g_own(0)
+    for h in (1, 0):
+        send(gh(c, h), gh(c, h), f"gy_0{h}", ypair)
     w_far(0)
-    g_step(0, 1)
-    w_two()
+    g_step(0, 1, 1)
+    g_step(0, 1, 0)
+    w_two(0)
+    g_step(0, 2, 1)
+    g_step(0, 2, 0)
+    w_two(1)
+    g_step(0, 3, 1)
+    build(f_ref, a_hi, a_lo, 0)
+    g_partner(1)
+    g_step(0, 3, 0)
+    g_partner(0)
+    w_far(1)
     w_near(0)
-    g_step(0, 2)
-    g_partner()
     w_last(0)
-    build(f_ref, a_hi, a_lo, 0)
-    w_far(1)
-    g_step(0, 3)
-    g_step(1, 1)
+    g_step(1, 1, 1)
+    g_step(0, 4, 1)
+    g_step(1, 1, 0)
+    g_step(0, 4, 0)
     w_near(1)
-    g_step(0, 4)
     w_last(1)
     own.wait()
+    og_copy.wait()
     for flip in (0, 1):
         recv(wp.at[rowid(0, flip, 1)], f"w_s0{flip}", sib)
         for d in (1, -1):
@@ -289,16 +306,24 @@
     def hrows(h):
         return pl.ds(h * half, half)
 
-    def p_pass(flip, dist):
+    def p_pass(flip, dist, parts=(0, 1)):
         far = 3 if flip else 4
-        for h in (0, 1):
+        for h in parts:
             for n, s in enumerate((1, -1)):
                 hh = 1 - h if s == 1 else h
                 rows = hrows(hh)
                 dest = colid(s * dist, flip)
                 if dist == 4 and hh != far_half(s):
                     continue
-                if dist < far and not (not flip and dist == 3 and hh != far_half(s)):
+                if flip and dist == 3 and hh == far_half(s):
+                    send(pb.at[dest, rows], py3.at[n], f"py_{s * 3}", ypair)
+                    continue
+                if not flip and dist == 3 and hh == far_half(s):
+                    recv(py3.at[n], f"py_{s * 3}", ypair)
+                    add_into(pb.at[dest, rows], py3.at[n])
+                whole = flip and dist == 2 and hh == far_half(s)
+                whole = whole or (not flip and dist == 3 and hh != far_half(s))
+                if dist < far and not whole:
                     recv(rp.at[n, flip, dist, rows], f"p_{s}_{flip}_{dist + 1}_{hh}", zdev[-s])
                     add_into(pb.at[dest, rows], rp.at[n, flip, dist, rows])
                 send(
@@ -306,14 +331,16 @@
                     f"p_{s}_{flip}_{dist}_{hh}", zdev[s],
                 )
 
-    lax.fori_loop(3, 6, partial, 0)
+    lax.fori_loop(2, 7, partial, 0)
     send(pb.at[colid(4, 1)], py, "py_4", ypair)
     p_pass(1, 3)
-    lax.fori_loop(6, 16, partial, 0)
-    lax.fori_loop(0, 3, partial, 0)
-    g_step(1, 2)
-    for d in (-3, 3, 4):
-        recv(gp.at[colid(d, 1)], f"gy_{d}", ypair)
+    p_pass(1, 2, (1,))
+    lax.fori_loop(12, 13, partial, 0)
+    for h in (1, 0):
+        g_step(1, 2, h)
+        for d in (-3, 3):
+            recv(gh(colid(-d, 1), h), f"gy_{d}_{h}", ypair)
+        recv(gh(colid(4, 1), h), f"gy_4_{h}", ypair)
 
     sib_base = slot("s_0")
     for i in range(1, 8):
@@ -347,16 +374,15 @@
             rows = w_half(s)
             send(wb.at[dest, rows], xfar.at[n, flip], f"x_far{s}_{flip}", xdev[s])
 
-    def wx_near(flip):
-        for late in (0, 1):
-            for n, s in enumerate((1, -1)):
-                dest = rowid(s, flip, 0)
-                h = far_half(s) if late else 1 - far_half(s)
-                rows = pl.ds(h * whalf, whalf)
-                if late:
-                    recv(xfar.at[n, flip], f"x_far{s}_{flip}", xdev[-s])
-                    add_into(wb.at[dest, rows], xfar.at[n, flip])
-                send(wb.at[dest, rows], xnear.at[n, flip, rows], f"x_near{s}_{flip}_{h}", xdev[s])
+    def wx_near(flip, late):
+        for n, s in enumerate((1, -1)):
+            dest = rowid(s, flip, 0)
+            h = far_half(s) if late else 1 - far_half(s)
+            rows = pl.ds(h * whalf, whalf)
+            if late:
+                recv(xfar.at[n, flip], f"x_far{s}_{flip}", xdev[-s])
+                add_into(wb.at[dest, rows], xfar.at[n, flip])
+            send(wb.at[dest, rows], xnear.at[n, flip, rows], f"x_near{s}_{flip}_{h}", xdev[s])
 
     def w_total(flip):
         dest = rowid(0, flip, 0)
@@ -370,23 +396,27 @@
         acc[...] += dot(gp[i], wp[i])
         return carry
 
-    lax.fori_loop(0, 4, for_sib, 0)
+    lax.fori_loop(0, 8, for_sib, 0)
     lax.fori_loop(0, 2, for_own, 0)
     wx_far(1)
     recv(py, "py_4", ypair)
     add_into(pb.at[colid(4, 0)], py)
     p_pass(0, 4)
-    lax.fori_loop(4, 8, for_sib, 0)
-    p_pass(1, 2)
-    lax.fori_loop(2, 8, for_own, 0)
-    wx_near(1)
+    p_pass(1, 2, (0,))
+    lax.fori_loop(2, 4, for_own, 0)
+    wx_near(1, 0)
+    lax.fori_loop(7, 12, partial, 0)
+    lax.fori_loop(13, 16, partial, 0)
+    lax.fori_loop(0, 2, partial, 0)
+    p_pass(0, 3)
+    lax.fori_loop(4, 8, for_own, 0)
+    wx_near(1, 1)
     wx_far(0)
-    p_pass(0, 3)
+    wx_near(0, 0)
     acc[...] = jnp.zeros_like(acc)
-    lax.fori_loop(0, 5, mix, 0)
+    lax.fori_loop(0, 4, mix, 0)
     p_pass(1, 1)
-    wx_near(0)
-    lax.fori_loop(5, 10, mix, 0)
+    lax.fori_loop(4, 7, mix, 0)
     p_pass(0, 2)
     blk = colid(0, 1)
     for h in (1, 0):
@@ -394,14 +424,18 @@
         for n, s in enumerate((1, -1)):
             recv(rp.at[n, 1, 0, rows], f"p_{s}_1_1_{h}", zdev[-s])
             add_into(pb.at[blk, rows], rp.at[n, 1, 0, rows])
-    send(pb.at[blk], pair, "py_0", ypair)
+        send(pb.at[blk, rows], pair.at[rows], f"py_0_{h}", ypair)
     w_total(1)
     send(wb.at[rowid(0, 1, 0)], yb, "x_y", ytwo)
+    wx_near(0, 1)
+    lax.fori_loop(7, 10, mix, 0)
     p_pass(0, 1)
     lax.fori_loop(10, 16, mix, 0)
     mixed_ref[...] = acc[...].astype(BF16)
-
-    recv(pair, "py_0", ypair)
+    results = [local(mixed_ref, mixed_out, 5)]
+
+    for h in (1, 0):
+        recv(pair.at[hrows(h)], f"py_0_{h}", ypair)
     step = 64
 
     def gradients(i, carry):
@@ -418,6 +452,8 @@
         lax.fori_loop(h * half // step, (h + 1) * half // step, gradients, 0)
         if h == 0:
             send(gc.at[pl.ds(0, span)], g_rim, "rim", before)
+
+    results.append(local(qg_ref, qg_out, 6))
 
     def corr(j, carry):
         cols = pl.ds(pl.multiple_of(j * lanes, lanes), lanes)
@@ -442,9 +478,9 @@
         return carry
 
     lax.fori_loop(0, tiles, corr, 0)
-    tin[x] = taps[...][:, 1:span + 1]
-    for d in (1, -1, 2):
-        send(tin.at[x], tin.at[x], f"t_{d}", xdev[d])
+    tin[r] = taps[...][:, 1:span + 1]
+    for k in (10, 6, 14, 2, 11, 5, 9, 7, 8, 15, 3, 13, 4, 12, 1):
+        send(tin.at[r], tin.at[r], f"t_{k}", (lax.rem(r + k, 16), c))
 
     def backward(j, carry):
         cols = pl.ds(pl.multiple_of(j * lanes, lanes), lanes)
@@ -465,22 +501,10 @@
         return carry
 
     recv(g_rim, "rim", after)
-    lax.fori_loop(0, tiles // 2, backward, 0)
-    for d in (1, -1, 2):
-        recv(tin.at[rowid(-d, 0, 0) // 4], f"t_{d}", xdev[-d if d != 2 else 2])
-    quad = yh * 2 + core
-    tin[4 + quad] = (tin[0] + tin[1]) + (tin[2] + tin[3])
-    mates = ((sib, yh * 2 + 1 - core), (ytwo, 2 - 2 * yh + core), (ysib, 3 - quad))
-    for n, (dev, _) in enumerate(mates):
-        send(tin.at[4 + quad], tin.at[4 + quad], f"t_q{n}", dev)
-    lax.fori_loop(tiles // 2, tiles, backward, 0)
-
+    lax.fori_loop(0, tiles, backward, 0)
+    results.append(local(kg_ref, kg_out, 7))
+    results.append(local(vg_ref, vg_out, 8))
     w_total(0)
-    for n, (dev, place) in enumerate(mates):
-        recv(tin.at[4 + place], f"t_q{n}", dev)
-    total = (tin[4] + tin[5]) + (tin[6] + tin[7])
-    fg_ref[...] = reversed_taps(total * (1.0 / math.sqrt(tok * 16 * group)))
-
     recv(yb, "x_y", ytwo)
     final = wb.at[r]
     scale = 1.0 / math.sqrt(tok * 16)
@@ -493,7 +517,7 @@
         return carry
 
     lax.fori_loop(0, wid // step, finish, 0)
-
+    results.append(local(wg_ref, wg_out, 9))
     for copy in started:
         copy.wait_send()
 
@@ -502,6 +526,16 @@
         return carry
 
     lax.fori_loop(0, 8, drain, 0)
+    for k in range(1, 16):
+        recv(tin.at[lax.rem(r + 16 - k, 16)], f"t_{k}", (lax.rem(r + 16 - k, 16), c))
+    total = tin[0]
+    for k in range(1, 16):
+        total += tin[k]
+    fg_ref[...] = reversed_taps(total * (1.0 / math.sqrt(tok * 16 * group)))
+
+    results.append(local(fg_ref, fg_out, 10))
+    for copy in results:
+        copy.wait()
     assert len(names) <= ss.shape[0], len(names)
 
 
@@ -523,7 +557,8 @@
     groups, span = filters.shape
     act = jax.ShapeDtypeStruct((tok, wid), BF16)
     vmem = pl.BlockSpec(memory_space=pltpu.VMEM)
-    sems = 120
+    anywhere = pl.BlockSpec(memory_space=pl.ANY)
+    sems = 144
     shapes = (
         act, act, act, act,
         jax.ShapeDtypeStruct((wid, wid), BF16),
@@ -532,9 +567,11 @@
     results = pl.pallas_call(
         kernel,
         out_shape=shapes,
-        in_specs=[vmem] * 6,
-        out_specs=[vmem] * 6,
-        scratch_shapes=[
+        in_specs=[anywhere] * 3 + [vmem] + [anywhere] * 2,
+        out_specs=[anywhere] * 6,
+        scratch_shapes=[pltpu.VMEM((tok, wid), BF16)] * 4
+        + [pltpu.VMEM(a.shape, a.dtype) for a in shapes]
+        + [
             pltpu.VMEM((span, wid), BF16),
             pltpu.VMEM((span, wid), BF16),
             pltpu.VMEM((span, wid), BF16),
@@ -552,6 +589,7 @@
             pltpu.VMEM((16, tok, wid), BF16),
             pltpu.VMEM((2, 2, 4, tok, wid), BF16),
             pltpu.VMEM((tok, wid), BF16),
+            pltpu.VMEM((2, tok // 2, wid), BF16),
             pltpu.VMEM((tok, wid), BF16),
             pltpu.VMEM((16, wid, wid), BF16),
             pltpu.VMEM((8, wid, wid), BF16),
@@ -559,17 +597,16 @@
             pltpu.VMEM((2, 2, wid, wid), BF16),
             pltpu.VMEM((wid, wid), BF16),
             pltpu.VMEM((groups, 2 * span), F32),
-            pltpu.VMEM((8, groups, span), F32),
+            pltpu.VMEM((16, groups, span), F32),
             pltpu.VMEM((tok, wid), F32),
             pltpu.SemaphoreType.DMA((sems,)),
             pltpu.SemaphoreType.DMA((sems,)),
-            pltpu.SemaphoreType.DMA((1,)),
+            pltpu.SemaphoreType.DMA((11,)),
         ],
         compiler_params=pltpu.CompilerParams(
             collective_id=0, has_side_effects=True, vmem_limit_bytes=67_000_000
         ),
     )(query_in, key_in, value_in, filters, out_weight, out_grad)
-    anywhere = pl.BlockSpec(memory_space=pl.ANY)
     return pl.pallas_call(
         relay,
         out_shape=shapes,

time: 119 us -> 106 us (0.89)
  Pallas kernels: 118 us -> 105 us
    pallas_call x1, Pallas kernels: 116 us -> 103 us  [shards(): pl.pallas_call(kernel, out_shape=shapes, in_specs=[anywhere] * 3 + [vmem]...]
where the time goes in v4:
time: 106 us
  Pallas kernels  105 us (99%)
    pallas_call x1, Pallas kernels, shards(): pl.pallas_call(kernel, out_shape=shapes, in_specs=[anywhere] * 3 + [vmem]...  103 us
    pallas_call x1, Pallas kernels, shards(): pl.pallas_call(relay, out_shape=shapes, in_specs=[anywhere] * 6, out_spec...  2.26 us

profile of v4, /device:TPU:1, one launch (start us, length us, event | category | flops | bytes accessed | tf_op | source)
XLA Modules:
  0.0 106.1 jit_solution(6453633683324504158)
XLA Ops:
  0.6 103.2 %shard_map.109 = (bf16[256,512]{1,0:T(8,128)(2,1)}, bf16[256,512]{1,0:T(8,128)(2,1)}, bf16[256,512]{1,0:T(8,128)(2,1)}, bf16[256,512]{1,0:T(8,128)(2,1)}, bf16[512,512]{1,0:T(8,128)(2,1)}, /*index=5*/f32[32,128]{1,0:T(8,128)}) custom-call(bf16[256,512]{1,0:T(8,128)(2,1)} %q_in.1, bf16[256,512]{1,0:T(8,128)(2,1)} %k_in.1, bf16[256,512]{1,0:T(8,128)(2,1)} %v_in.1, ...), custom_call_target="tpu_custom_call" | custom-call | tf_op jit(solution)/shard_map/pallas_call | solution.py:567
  103.8 2.3 %shard_map.110 = (bf16[256,512]{1,0:T(8,128)(2,1)}, bf16[256,512]{1,0:T(8,128)(2,1)}, bf16[256,512]{1,0:T(8,128)(2,1)}, bf16[256,512]{1,0:T(8,128)(2,1)}, bf16[512,512]{1,0:T(8,128)(2,1)}, /*index=5*/f32[32,128]{1,0:T(8,128)}) custom-call(bf16[256,512]{1,0:T(8,128)(2,1)} %get-tuple-element.12.refs_0_, bf16[256,512]{1,0:T(8,128)(2,1)} %get-tuple-element.13.refs_1_, ...), custom_call_target="tpu_custom_call" | custom-call | tf_op jit(solution)/shard_map/pallas_call | solution.py:610
